TPU v7x, 32 devices: a whole 2x2x4 slice. The times are simulated.
32 devices in a mesh: dp: 2 (over x), row: 4 (over y, core), col: 4 (over z).
Axes of the slice: x: 2, y: 2, z: 4, core: 2. Of those that a mesh axis runs over, the one named last changes fastest.
Arguments:
- images: bfloat16 [2, 2, 64, 64, 768], P(None, 'dp', 'row', 'col'), may hold values from -6 to 6
- qkv_weight: bfloat16 [768, 2304], P(('dp', 'row', 'col')), may hold values from -0.21875 to 0.21875
- qv_bias: bfloat16 [1536], P(('dp', 'row', 'col')), may hold values from -1.5 to 1.5
- proj_weight: bfloat16 [768, 768], P(('dp', 'row', 'col')), may hold values from -1.5 to 1.5
- proj_bias: bfloat16 [768], P(('dp', 'row', 'col')), may hold values from -1.5 to 1.5
- pre_gain: bfloat16 [768], P(('dp', 'row', 'col')), may hold values from 0.5 to 1.5
- pre_shift: bfloat16 [768], P(('dp', 'row', 'col')), may hold values from -1.5 to 1.5
- mid_gain: bfloat16 [768], P(('dp', 'row', 'col')), may hold values from 0.5 to 1.5
- mid_shift: bfloat16 [768], P(('dp', 'row', 'col')), may hold values from -1.5 to 1.5
- up_weight: bfloat16 [768, 3072], P(('dp', 'row', 'col')), may hold values from -0.21875 to 0.21875
- up_bias: bfloat16 [3072], P(('dp', 'row', 'col')), may hold values from -1.5 to 1.5
- down_weight: bfloat16 [3072, 768], P(('dp', 'row', 'col')), may hold values from -0.109375 to 0.109375
- down_bias: bfloat16 [768], P(('dp', 'row', 'col')), may hold values from -1.5 to 1.5
- rel_rows: bfloat16 [27, 64], replicated, may hold values from -0.5 to 0.5
- rel_cols: bfloat16 [27, 64], replicated, may hold values from -0.5 to 0.5
- cotangent: bfloat16 [2, 2, 64, 64, 768], P(None, 'dp', 'row', 'col'), may hold values from -6 to 6
Outputs:
- out: bfloat16 [2, 2, 64, 64, 768], P(None, 'dp', 'row', 'col')
- images_grad: float32 [2, 2, 64, 64, 768], P(None, 'dp', 'row', 'col')
- qkv_weight_grad: float32 [768, 2304], P(('dp', 'row', 'col'))
- qv_bias_grad: float32 [1536], P(('dp', 'row', 'col'))
- proj_weight_grad: float32 [768, 768], P(('dp', 'row', 'col'))
- proj_bias_grad: float32 [768], P(('dp', 'row', 'col'))
- pre_gain_grad: float32 [768], P(('dp', 'row', 'col'))
- pre_shift_grad: float32 [768], P(('dp', 'row', 'col'))
- mid_gain_grad: float32 [768], P(('dp', 'row', 'col'))
- mid_shift_grad: float32 [768], P(('dp', 'row', 'col'))
- up_weight_grad: float32 [768, 3072], P(('dp', 'row', 'col'))
- up_bias_grad: float32 [3072], P(('dp', 'row', 'col'))
- down_weight_grad: float32 [3072, 768], P(('dp', 'row', 'col'))
- down_bias_grad: float32 [768], P(('dp', 'row', 'col'))
- rel_rows_grad: float32 [27, 64], replicated
- rel_cols_grad: float32 [27, 64], replicated
All inputs are finite; a program needn't handle non-finite values.
Results may differ from a plain program's by a relative error of at most 0.013.
Values may be sent and summed in bfloat16 or wider, within the bound.
No kernel may reach another device: no remote copies, remote signals or barrier semaphores. Data moves between devices by JAX's collectives and lax.ppermute only.
A program may use at most 384 MiB of HBM per device.

v0:
```python
import math

import jax
import jax.numpy as jnp
from jax import lax
from jax.sharding import PartitionSpec as P

HEAD = 64
WIN = 14
NWIN = 5


epsilon = 1e-06
exact_prec = lax.Precision.HIGHEST


def shifted(value, axis, steps):
    count = lax.axis_size(axis)
    first, last = (max(0, -steps), min(count, count - steps))
    return lax.ppermute(value, axis, [(source, source + steps) for source in range(first, last)])


def layer_norm(values, gain_vec, shift_vec):
    center = values - jnp.mean(values, axis=-1, keepdims=True)
    inverse = lax.rsqrt(jnp.mean(center * center, axis=-1, keepdims=True) + epsilon)
    normed = center * inverse
    return (normed * gain_vec + shift_vec, normed, inverse)


def norm_back(upstream, normed, inverse, gain_vec):
    scaled = upstream * gain_vec
    inner_mean = jnp.mean(scaled, axis=-1, keepdims=True)
    cross_mean = jnp.mean(scaled * normed, axis=-1, keepdims=True)
    result = inverse * (scaled - inner_mean - normed * cross_mean)
    return (result, jnp.sum(upstream * normed, axis=0), jnp.sum(upstream, axis=0))


def offset_onehot(kind):
    shape_three = (WIN, WIN, 2 * WIN - 1)
    places = (
        lax.broadcasted_iota(jnp.int32, shape_three, 0)
        - lax.broadcasted_iota(jnp.int32, shape_three, 1)
        + WIN
        - 1
    )
    return (places == lax.broadcasted_iota(jnp.int32, shape_three, 2)).astype(kind)


def expand_table(table_rows):
    return jnp.einsum(
        "xkr,rc->xkc", offset_onehot(jnp.bfloat16), table_rows, preferred_element_type=jnp.float32
    )


def fold_table(table_grad):
    return jnp.einsum("xkr,xkc->rc", offset_onehot(jnp.float32), table_grad, precision=exact_prec)


def extend(tile):
    tile_rows = tile.shape[1]
    tile_cols = tile.shape[2]
    reach_rows = (WIN + tile_rows - 2) // tile_rows
    reach_cols = (WIN + tile_cols - 2) // tile_cols
    pieces = [tile]
    offset = 0
    pieces.append(shifted(tile, "row", -(offset + 1)))
    tall = jnp.concatenate(pieces, axis=1)
    pieces = [tall]
    for offset in range(reach_cols):
        pieces.append(shifted(tall, "col", -(offset + 1)))
    return jnp.concatenate(pieces, axis=2)


def fold_back(buffer, tile_rows, tile_cols):
    reach_rows = buffer.shape[1] // tile_rows - 1
    reach_cols = buffer.shape[2] // tile_cols - 1
    merged = buffer[:, :, :tile_cols]
    for offset in range(reach_cols):
        column_part = buffer[:, :, (offset + 1) * tile_cols : (offset + 2) * tile_cols]
        merged = merged + shifted(column_part, "col", offset + 1)
    result = merged[:, :tile_rows]
    offset = 0
    row_part = merged[:, (offset + 1) * tile_rows : (offset + 2) * tile_rows]
    result = result + shifted(row_part, "row", offset + 1)
    return result


def window_slots(tile_rows, tile_cols):
    row_index = lax.axis_index("row")
    col_index = lax.axis_index("col")
    first_row = (tile_rows * row_index + WIN - 1) // WIN
    first_col = (tile_cols * col_index + WIN - 1) // WIN
    slot_list = []
    for slot_row in range((tile_rows + WIN - 1) // WIN):
        for slot_col in range((tile_cols + WIN - 1) // WIN):
            win_row = first_row + slot_row
            win_col = first_col + slot_col
            usable = (WIN * win_row < tile_rows * (row_index + 1)) & (win_row < NWIN)
            usable = usable & (WIN * win_col < tile_cols * (col_index + 1)) & (win_col < NWIN)
            slot_list.append(
                (
                    WIN * win_row - tile_rows * row_index,
                    WIN * win_col - tile_cols * col_index,
                    usable,
                )
            )
    return slot_list


def cut_windows(extended, slot_list):
    images_here = extended.shape[0]
    model_width = extended.shape[3]
    blocks = []
    for start_row, start_col, usable in slot_list:
        blocks.append(
            lax.dynamic_slice(
                extended, (0, start_row, start_col, 0), (images_here, WIN, WIN, model_width)
            )
        )
    return jnp.stack(blocks, axis=1).reshape(-1, WIN * WIN, model_width)


def place_windows(windows, slot_list, shape_like):
    images_here = shape_like.shape[0]
    grouped = windows.reshape(images_here, len(slot_list), WIN, WIN, windows.shape[-1])
    buffer = jnp.zeros(shape_like.shape, windows.dtype)
    for number, (start_row, start_col, usable) in enumerate(slot_list):
        updated = lax.dynamic_update_slice(buffer, grouped[:, number], (0, start_row, start_col, 0))
        buffer = jnp.where(usable, updated, buffer)
    return buffer


def window_scores(queries, key_rows, row_table, col_table):
    window_count = queries.shape[0]
    heads_here = queries.shape[2]
    head_size = queries.shape[3]
    scores = jnp.einsum(
        "nqhc,nkhc->nhqk", queries, key_rows, preferred_element_type=jnp.float32
    ) * head_size ** (-0.5)
    grid_queries = queries.reshape(window_count, WIN, WIN, heads_here, head_size)
    along_rows = jnp.einsum(
        "nxyhc,xkc->nhxyk",
        grid_queries,
        row_table.astype(jnp.bfloat16),
        preferred_element_type=jnp.float32,
    )
    along_cols = jnp.einsum(
        "nxyhc,ykc->nhxyk",
        grid_queries,
        col_table.astype(jnp.bfloat16),
        preferred_element_type=jnp.float32,
    )
    scores = (
        scores.reshape(window_count, heads_here, WIN, WIN, WIN, WIN)
        + along_rows[..., :, None]
        + along_cols[..., None, :]
    )
    return scores.reshape(window_count, heads_here, WIN * WIN, WIN * WIN)


def attention_back(queries, key_rows, value_rows, row_table, col_table, logsum, upstream):
    window_count = queries.shape[0]
    heads_here = queries.shape[2]
    head_size = queries.shape[3]
    scores = window_scores(queries, key_rows, row_table, col_table)
    attention = jnp.exp(scores - logsum[..., None])
    value_grad = jnp.einsum(
        "nhqk,nqhc->nkhc",
        attention.astype(jnp.bfloat16),
        upstream,
        preferred_element_type=jnp.float32,
    )
    attention_grad = jnp.einsum(
        "nqhc,nkhc->nhqk", upstream, value_rows, preferred_element_type=jnp.float32
    )
    score_grad = attention * (
        attention_grad - jnp.sum(attention * attention_grad, axis=-1, keepdims=True)
    )
    score_grad = score_grad.astype(jnp.bfloat16)
    factor = head_size ** (-0.5)
    query_grad = (
        jnp.einsum("nhqk,nkhc->nqhc", score_grad, key_rows, preferred_element_type=jnp.float32)
        * factor
    )
    key_grad = (
        jnp.einsum("nhqk,nqhc->nkhc", score_grad, queries, preferred_element_type=jnp.float32)
        * factor
    )
    split_grad = score_grad.reshape(window_count, heads_here, WIN, WIN, WIN, WIN)
    row_sums = jnp.sum(split_grad, axis=5, dtype=jnp.float32)
    col_sums = jnp.sum(split_grad, axis=4, dtype=jnp.float32)
    rel_part = jnp.einsum("nhxyk,xkc->nxyhc", row_sums, row_table, precision=exact_prec)
    rel_part = rel_part + jnp.einsum("nhxyk,ykc->nxyhc", col_sums, col_table, precision=exact_prec)
    query_grad = query_grad + rel_part.reshape(window_count, WIN * WIN, heads_here, head_size)
    grid_queries = queries.astype(jnp.float32).reshape(
        window_count, WIN, WIN, heads_here, head_size
    )
    row_table_grad = jnp.einsum("nhxyk,nxyhc->xkc", row_sums, grid_queries, precision=exact_prec)
    col_table_grad = jnp.einsum("nhxyk,nxyhc->ykc", col_sums, grid_queries, precision=exact_prec)
    return (
        query_grad,
        key_grad,
        value_grad,
        fold_table(row_table_grad),
        fold_table(col_table_grad),
    )


def micro_step(pixels, incoming, gathered, row_table, col_table, slot_list, window_mask):
    (
        qkv_full,
        qv_full,
        proj_full,
        proj_add,
        pre_scale,
        pre_add,
        mid_scale,
        mid_add,
        up_full,
        up_add,
        down_full,
        down_add,
    ) = gathered
    images_here, tile_rows, tile_cols, model_width = pixels.shape
    heads_here = model_width // HEAD
    tokens = pixels.reshape(-1, model_width).astype(jnp.float32)
    pre_scale_f = pre_scale.astype(jnp.float32)
    mid_scale_f = mid_scale.astype(jnp.float32)
    normed_one, plain_one, inverse_one = layer_norm(
        tokens, pre_scale_f, pre_add.astype(jnp.float32)
    )
    hidden = normed_one.astype(jnp.bfloat16).reshape(pixels.shape)
    extended = extend(hidden)
    windows = cut_windows(extended, slot_list)
    window_count = windows.shape[0]
    flat_windows = windows.reshape(-1, model_width)
    full_bias = jnp.concatenate(
        [qv_full[:model_width], jnp.zeros((model_width,), jnp.bfloat16), qv_full[model_width:]]
    )
    projected = jnp.dot(
        flat_windows, qkv_full, preferred_element_type=jnp.float32
    ) + full_bias.astype(jnp.float32)
    projected = projected.astype(jnp.bfloat16).reshape(window_count, WIN * WIN, 3, heads_here, HEAD)
    queries = projected[:, :, 0]
    key_rows = projected[:, :, 1]
    value_rows = projected[:, :, 2]
    scores = window_scores(queries, key_rows, row_table, col_table)
    peak = jnp.max(scores, axis=-1, keepdims=True)
    exp_scores = jnp.exp(scores - peak)
    total_mass = jnp.sum(exp_scores, axis=-1, keepdims=True)
    logsum = (peak + jnp.log(total_mass))[..., 0]
    attention = (exp_scores / total_mass).astype(jnp.bfloat16)
    attended = jnp.einsum(
        "nhqk,nkhc->nqhc", attention, value_rows, preferred_element_type=jnp.float32
    )
    attended = attended.astype(jnp.bfloat16).reshape(window_count, WIN * WIN, model_width)
    returned = fold_back(place_windows(attended, slot_list, extended), tile_rows, tile_cols)
    flat_attended = returned.reshape(-1, model_width)
    middle = (
        tokens
        + jnp.dot(flat_attended, proj_full, preferred_element_type=jnp.float32)
        + proj_add.astype(jnp.float32)
    )
    normed_two, plain_two, inverse_two = layer_norm(
        middle, mid_scale_f, mid_add.astype(jnp.float32)
    )
    second = normed_two.astype(jnp.bfloat16)
    inner_act = jnp.dot(second, up_full, preferred_element_type=jnp.float32) + up_add.astype(
        jnp.float32
    )
    active = jax.nn.gelu(inner_act, approximate=False).astype(jnp.bfloat16)
    result = (
        middle
        + jnp.dot(active, down_full, preferred_element_type=jnp.float32)
        + down_add.astype(jnp.float32)
    )
    output = result.astype(jnp.bfloat16).reshape(pixels.shape)
    upstream = incoming.reshape(-1, model_width)
    up_flow = upstream.astype(jnp.float32)
    down_weight_grad = jnp.einsum("tf,td->fd", active, upstream, preferred_element_type=jnp.float32)
    down_bias_grad = jnp.sum(up_flow, axis=0)
    active_grad = jnp.einsum("td,fd->tf", upstream, down_full, preferred_element_type=jnp.float32)
    cdf_part = 0.5 * (1.0 + lax.erf(inner_act * 2.0 ** (-0.5)))
    pdf_part = jnp.exp(-0.5 * inner_act * inner_act) * (2.0 * math.pi) ** (-0.5)
    inner_grad = (active_grad * (cdf_part + inner_act * pdf_part)).astype(jnp.bfloat16)
    up_weight_grad = jnp.einsum("td,tf->df", second, inner_grad, preferred_element_type=jnp.float32)
    up_bias_grad = jnp.sum(inner_grad, axis=0, dtype=jnp.float32)
    second_grad = jnp.einsum("tf,df->td", inner_grad, up_full, preferred_element_type=jnp.float32)
    middle_part, mid_gain_grad, mid_shift_grad = norm_back(
        second_grad, plain_two, inverse_two, mid_scale_f
    )
    middle_grad = up_flow + middle_part
    branch_grad = middle_grad.astype(jnp.bfloat16)
    proj_weight_grad = jnp.einsum(
        "td,te->de", flat_attended, branch_grad, preferred_element_type=jnp.float32
    )
    proj_bias_grad = jnp.sum(branch_grad, axis=0, dtype=jnp.float32)
    attended_grad = jnp.einsum(
        "te,de->td", branch_grad, proj_full, preferred_element_type=jnp.float32
    )
    attended_grad = attended_grad.astype(jnp.bfloat16).reshape(pixels.shape)
    window_grad = cut_windows(extend(attended_grad), slot_list) * window_mask
    window_grad = window_grad.reshape(window_count, WIN * WIN, heads_here, HEAD)
    query_grad, key_grad, value_grad, rel_rows_grad, rel_cols_grad = attention_back(
        queries, key_rows, value_rows, row_table, col_table, logsum, window_grad
    )
    projected_grad = jnp.stack([query_grad, key_grad, value_grad], axis=2).astype(jnp.bfloat16)
    projected_grad = projected_grad.reshape(-1, 3 * model_width)
    qkv_weight_grad = jnp.einsum(
        "td,te->de", flat_windows, projected_grad, preferred_element_type=jnp.float32
    )
    column_sums = jnp.sum(projected_grad, axis=0, dtype=jnp.float32)
    qv_bias_grad = jnp.concatenate([column_sums[:model_width], column_sums[2 * model_width :]])
    hidden_grad = jnp.einsum(
        "te,de->td", projected_grad, qkv_full, preferred_element_type=jnp.float32
    )
    hidden_grad = hidden_grad.astype(jnp.bfloat16).reshape(window_count, WIN * WIN, model_width)
    hidden_back = fold_back(place_windows(hidden_grad, slot_list, extended), tile_rows, tile_cols)
    first_part, pre_gain_grad, pre_shift_grad = norm_back(
        hidden_back.reshape(-1, model_width).astype(jnp.float32),
        plain_one,
        inverse_one,
        pre_scale_f,
    )
    input_grad = (middle_grad + first_part).reshape(pixels.shape)
    weight_grads = (
        qkv_weight_grad,
        qv_bias_grad,
        proj_weight_grad,
        proj_bias_grad,
        pre_gain_grad,
        pre_shift_grad,
        mid_gain_grad,
        mid_shift_grad,
        up_weight_grad,
        up_bias_grad,
        down_weight_grad,
        down_bias_grad,
    )
    return (output, input_grad, (weight_grads, (rel_rows_grad, rel_cols_grad)))


def fetch(shards):
    (
        qkv_weight,
        qv_bias,
        proj_weight,
        proj_bias,
        pre_gain,
        pre_shift,
        mid_gain,
        mid_shift,
        up_weight,
        up_bias,
        down_weight,
        down_bias,
    ) = shards
    return (
        lax.all_gather(qkv_weight, ("dp", "row", "col"), axis=0, tiled=True),
        lax.all_gather(qv_bias, ("dp", "row", "col"), axis=0, tiled=True),
        lax.all_gather(proj_weight, ("dp", "row", "col"), axis=0, tiled=True),
        lax.all_gather(proj_bias, ("dp", "row", "col"), axis=0, tiled=True),
        lax.all_gather(pre_gain, ("dp", "row", "col"), axis=0, tiled=True),
        lax.all_gather(pre_shift, ("dp", "row", "col"), axis=0, tiled=True),
        lax.all_gather(mid_gain, ("dp", "row", "col"), axis=0, tiled=True),
        lax.all_gather(mid_shift, ("dp", "row", "col"), axis=0, tiled=True),
        lax.all_gather(up_weight, ("dp", "row", "col"), axis=0, tiled=True),
        lax.all_gather(up_bias, ("dp", "row", "col"), axis=0, tiled=True),
        lax.all_gather(down_weight, ("dp", "row", "col"), axis=0, tiled=True),
        lax.all_gather(down_bias, ("dp", "row", "col"), axis=0, tiled=True),
    )


def reduce_grads(local):
    weight_grads, table_pair = local
    (
        grad_qkv,
        grad_qv,
        grad_proj,
        grad_proj_add,
        grad_pre_scale,
        grad_pre_add,
        grad_mid_scale,
        grad_mid_add,
        grad_up,
        grad_up_add,
        grad_down,
        grad_down_add,
    ) = weight_grads
    row_grad, col_grad = table_pair
    shares = (
        lax.psum_scatter(grad_qkv, ("dp", "row", "col"), scatter_dimension=0, tiled=True),
        lax.psum_scatter(grad_qv, ("dp", "row", "col"), scatter_dimension=0, tiled=True),
        lax.psum_scatter(grad_proj, ("dp", "row", "col"), scatter_dimension=0, tiled=True),
        lax.psum_scatter(grad_proj_add, ("dp", "row", "col"), scatter_dimension=0, tiled=True),
        lax.psum_scatter(grad_pre_scale, ("dp", "row", "col"), scatter_dimension=0, tiled=True),
        lax.psum_scatter(grad_pre_add, ("dp", "row", "col"), scatter_dimension=0, tiled=True),
        lax.psum_scatter(grad_mid_scale, ("dp", "row", "col"), scatter_dimension=0, tiled=True),
        lax.psum_scatter(grad_mid_add, ("dp", "row", "col"), scatter_dimension=0, tiled=True),
        lax.psum_scatter(grad_up, ("dp", "row", "col"), scatter_dimension=0, tiled=True),
        lax.psum_scatter(grad_up_add, ("dp", "row", "col"), scatter_dimension=0, tiled=True),
        lax.psum_scatter(grad_down, ("dp", "row", "col"), scatter_dimension=0, tiled=True),
        lax.psum_scatter(grad_down_add, ("dp", "row", "col"), scatter_dimension=0, tiled=True),
    )
    tables = lax.psum((row_grad, col_grad), ("dp", "row", "col"))
    return (tuple(shares), tuple(tables))


def body(
    images,
    qkv_weight,
    qv_bias,
    proj_weight,
    proj_bias,
    pre_gain,
    pre_shift,
    mid_gain,
    mid_shift,
    up_weight,
    up_bias,
    down_weight,
    down_bias,
    rel_rows,
    rel_cols,
    cotangent,
):
    shards = (
        qkv_weight,
        qv_bias,
        proj_weight,
        proj_bias,
        pre_gain,
        pre_shift,
        mid_gain,
        mid_shift,
        up_weight,
        up_bias,
        down_weight,
        down_bias,
    )
    micro_count = images.shape[0]
    images_here = images.shape[1]
    slot_list = window_slots(images.shape[2], images.shape[3])
    usable_vec = jnp.stack([entry[2] for entry in slot_list]).astype(jnp.bfloat16)
    window_mask = usable_vec[None, :].reshape(-1, 1, 1)
    row_table = expand_table(rel_rows)
    col_table = expand_table(rel_cols)
    reduced = None
    outputs = []
    input_grads = []
    for micro in range(micro_count):
        gathered = fetch(shards)
        output, input_grad, local = micro_step(
            images[micro], cotangent[micro], gathered, row_table, col_table, slot_list, window_mask
        )
        outputs.append(output)
        input_grads.append(input_grad)
        shared = reduce_grads(local)
        reduced = shared if reduced is None else jax.tree.map(jnp.add, reduced, shared)
    shares, tables = reduced
    return (
        jnp.stack(outputs, axis=0),
        jnp.stack(input_grads, axis=0),
        shares[0],
        shares[1],
        shares[2],
        shares[3],
        shares[4],
        shares[5],
        shares[6],
        shares[7],
        shares[8],
        shares[9],
        shares[10],
        shares[11],
        tables[0],
        tables[1],
    )


def solution(mesh):
    placed = (
        P(None, "dp", "row", "col", None),
        P(("dp", "row", "col"), None),
        P(("dp", "row", "col")),
        P(("dp", "row", "col"), None),
        P(("dp", "row", "col")),
        P(("dp", "row", "col")),
        P(("dp", "row", "col")),
        P(("dp", "row", "col")),
        P(("dp", "row", "col")),
        P(("dp", "row", "col"), None),
        P(("dp", "row", "col")),
        P(("dp", "row", "col"), None),
        P(("dp", "row", "col")),
        P(),
        P(),
        P(None, "dp", "row", "col", None),
    )
    return jax.shard_map(
        body,
        mesh=mesh,
        in_specs=placed,
        out_specs=(
            P(None, "dp", "row", "col", None),
            P(None, "dp", "row", "col", None),
            P(("dp", "row", "col"), None),
            P(("dp", "row", "col")),
            P(("dp", "row", "col"), None),
            P(("dp", "row", "col")),
            P(("dp", "row", "col")),
            P(("dp", "row", "col")),
            P(("dp", "row", "col")),
            P(("dp", "row", "col")),
            P(("dp", "row", "col"), None),
            P(("dp", "row", "col")),
            P(("dp", "row", "col"), None),
            P(("dp", "row", "col")),
            P(),
            P(),
        ),
        check_vma=False,
    )
```

profile of v0, /device:TPU:0, one launch (start us, length us, event | category | flops | bytes accessed | tf_op | source)
XLA Modules:
  0.0 1602.8 jit_solution(4063775440660362244)
XLA Ops:
  16.2 42.9 %all-reduce.17 = (bf16[768]{0:T(1024)(128)(2,1)S(1)}, bf16[768]{0:T(1024)(128)(2,1)S(1)}, bf16[1536]{0:T(1024)(128)(2,1)S(1)}, bf16[768]{0:T(1024)(128)(2,1)S(1)...) all-reduce(bf16[768]{0:T(1024)(128)(2,1)S(1)} %dynamic-update-slice, ...), channel_id=1, replica_groups=mesh['dp'=2,'row'=4,'col'=4] {'dp','row','col'}, use_global_device_ids=true, to_apply=%add.1 | all-reduce | flops 9216 | bytes 36864
  74.3 13.8 collective-permute-done.1
  90.8 15.5 collective-permute-done.5
  116.9 11.9 reshape.673
  149.9 11.9 reshape.674
  178.8 8.9 fusion.75
  187.7 8.9 fusion.72
  196.6 9.4 fusion.81
  205.9 8.9 fusion.78
  223.2 8.6 copy.403
  246.8 9.1 copy.416
  263.7 27.6 %add.526 = f32[4,12,14,14,14,14]{5,4,3,2,1,0:T(8,128)} broadcast(f32[4,12,14,14,14]{4,3,2,1,0:T(8,128)} %copy.413), dimensions={0,1,2,3,4} | broadcast | bytes 7902720 | tf_op jit(solution)/shard_map/add | solution.py:154
  291.3 44.6 %add.527 = f32[4,12,196,196]{3,2,1,0:T(8,128)} reshape(f32[4,12,14,14,14,14]{5,4,3,2,1,0:T(8,128)} %add.526) | data formatting | bytes 14751744 | tf_op jit(solution)/shard_map/add | solution.py:154
  335.9 11.2 copy.414
  347.1 26.0 %add.529 = f32[4,12,14,14,14,14]{5,4,3,2,1,0:T(8,128)} broadcast(f32[4,12,14,14,14]{4,3,2,1,0:T(8,128)} %copy.416), dimensions={0,1,2,3,5} | broadcast | bytes 7902720 | tf_op jit(solution)/shard_map/add | solution.py:154
  373.1 44.6 %add.530 = f32[4,12,196,196]{3,2,1,0:T(8,128)} reshape(f32[4,12,14,14,14,14]{5,4,3,2,1,0:T(8,128)} %add.529) | data formatting | bytes 14751744 | tf_op jit(solution)/shard_map/add | solution.py:154
  417.6 11.3 copy.417
  428.9 8.1 fusion.227
  483.0 28.0 %add.504 = f32[4,12,14,14,14,14]{5,4,3,2,1,0:T(8,128)} broadcast(f32[4,12,14,14,14]{4,3,2,1,0:T(8,128)} %copy.399), dimensions={0,1,2,3,4} | broadcast | bytes 7902720 | tf_op jit(solution)/shard_map/add | solution.py:154
  511.1 44.6 %add.505 = f32[4,12,196,196]{3,2,1,0:T(8,128)} reshape(f32[4,12,14,14,14,14]{5,4,3,2,1,0:T(8,128)} %add.504) | data formatting | bytes 14751744 | tf_op jit(solution)/shard_map/add | solution.py:154
  555.6 11.3 copy.400
  566.9 26.0 %add.507 = f32[4,12,14,14,14,14]{5,4,3,2,1,0:T(8,128)} broadcast(f32[4,12,14,14,14]{4,3,2,1,0:T(8,128)} %copy.403), dimensions={0,1,2,3,5} | broadcast | bytes 7902720 | tf_op jit(solution)/shard_map/add | solution.py:154
  592.9 44.6 %add.508 = f32[4,12,196,196]{3,2,1,0:T(8,128)} reshape(f32[4,12,14,14,14,14]{5,4,3,2,1,0:T(8,128)} %add.507) | data formatting | bytes 14751744 | tf_op jit(solution)/shard_map/add | solution.py:154
  637.5 11.3 copy.404
  648.8 7.9 fusion.229
  710.9 9.4 collective-permute-done.2
  731.6 11.2 fusion.32
  752.2 9.2 fusion.35
  782.9 10.1 collective-permute-done.13
  807.4 8.4 multiply_reduce_fusion
  815.8 11.5 multiply_convert_fusion
  832.6 8.6 copy.443
  860.4 8.8 multiply_reduce_fusion.1
  869.3 11.6 multiply_convert_fusion.1
  880.8 8.5 copy.428
  889.3 43.0 %reshape.639 = f32[4,12,14,14,14,14]{5,4,3,2,1,0:T(8,128)} reshape(f32[4,12,196,196]{3,2,1,0:T(8,128)} %copy.428) | data formatting | bytes 14751744 | tf_op jit(solution)/shard_map/convert_element_type | solution.py:190
  932.3 43.1 %reshape.641 = f32[4,12,14,14,14,14]{5,4,3,2,1,0:T(8,128)} reshape(f32[4,12,196,196]{3,2,1,0:T(8,128)} %copy.443) | data formatting | bytes 14751744 | tf_op jit(solution)/shard_map/convert_element_type | solution.py:190
  975.4 66.7 %fusion.217 = (f32[4,12,14,14,14]{4,3,2,1,0:T(8,128)}, f32[4,12,14,14,14]{4,3,2,1,0:T(8,128)}, f32[4,12,14,14,14]{4,3,2,1,0:T(8,128)}, f32[4,12,14,14,14]{4,3,2,1,0:T(8,128)}) fusion(f32[4,12,14,14,14,14]{5,4,3,2,1,0:T(8,128)} %reshape.639, f32[4,12,14,14,14,14]{5,4,3,2,1,0:T(8,128)} %reshape.641), kind=kLoop, calls=%fused_computation.359 | loop fusion | flops 6849024 | bytes 16859136 | tf_op jit(solution)/shard_map/reduce_sum | solution.py:190
  1042.1 9.5 fusion.16
  1051.7 8.1 bitcast_add_fusion.1
  1084.9 8.3 bitcast_add_fusion
  1118.4 9.7 convert_element_type.375
  1146.8 9.7 convert_element_type.361
  1287.6 9.3 fusion.137
  1298.3 13.4 collective-permute-start.15
  1317.4 44.2 %all-reduce.16 = (f32[1536]{0:T(1024)S(1)}, f32[768]{0:T(1024)S(1)}, f32[768]{0:T(1024)S(1)}, f32[768]{0:T(1024)S(1)}, f32[768]{0:T(1024)S(1)}, /*index=5*/f32[7...) all-reduce(f32[1536]{0:T(1024)S(1)} %maximum_add_fusion, ...), channel_id=15, replica_groups=mesh['dp'=2,'row'=4,'col'=4] {'dp','row','col'}, use_global_device_ids=true, to_apply=%region_29.30.clone | all-reduce | flops 12672 | bytes 101376
  1368.6 85.0 %reduce-scatter.9.cloned.1.call-done = f32[24,3072]{1,0:T(8,128)} async-done(((f32[768,3072]{1,0:T(8,128)}), f32[24,3072]{1,0:T(8,128)}) %reduce-scatter.9.cloned.1.call-update) | async-done | bytes 294928 | tf_op jit(solution)/shard_map/reduce_scatter | solution.py:400
  1453.5 142.2 %reduce-scatter.11.cloned.1.call-done = f32[96,768]{1,0:T(8,128)} async-done(((f32[3072,768]{1,0:T(8,128)}), f32[96,768]{1,0:T(8,128)}) %reduce-scatter.11.cloned.1.call-update) | async-done | bytes 294928 | tf_op jit(solution)/shard_map/reduce_scatter | solution.py:402
  (568 shorter events, 499.7 us)
Async XLA Ops:
  7.2 61.6 %copy-start = (bf16[27,64]{1,0:T(8,128)(2,1)S(1)}, bf16[27,64]{1,0:T(8,128)(2,1)}, u32[]{:S(2)}) copy-start(bf16[27,64]{1,0:T(8,128)(2,1)} %param.30) | copy-start | bytes 10372
  7.2 63.2 %copy-start.117 = (bf16[27,64]{1,0:T(8,128)(2,1)S(1)}, bf16[27,64]{1,0:T(8,128)(2,1)}, u32[]{:S(2)}) copy-start(bf16[27,64]{1,0:T(8,128)(2,1)} %param.29) | copy-start | bytes 10372
  7.2 102.5 %all-gather.5.cloned.1.call-start = ((), (), s32[]{:S(2)}) async-start(), calls=%async_computation.4 | async-start | bytes 3649536 | tf_op jit(solution)/shard_map/all_gather | solution.py:359
  7.9 716.5 %all-gather.7.cloned.1.call-start = ((), (), s32[]{:S(2)}) async-start(), calls=%async_computation.5 | async-start | bytes 1216512 | tf_op jit(solution)/shard_map/all_gather | solution.py:361
  8.7 722.9 %all-gather.9.cloned.1.call-start = ((), (), s32[]{:S(2)}) async-start(), calls=%async_computation.6 | async-start | bytes 4866048 | tf_op jit(solution)/shard_map/all_gather | solution.py:367
  9.4 733.4 %all-gather.11.cloned.1.call-start = ((), (), s32[]{:S(2)}) async-start(), calls=%async_computation.7 | async-start | bytes 4866048 | tf_op jit(solution)/shard_map/all_gather | solution.py:369
  63.6 5.4 collective-permute-start
  64.9 5.7 collective-permute-start.4
  66.2 1302.4 %reduce-scatter.7.cloned.1.call-start = ((), (), s32[]{:S(2)}) async-start(), calls=%async_computation.9 | async-start | bytes 2433024 | tf_op jit(solution)/shard_map/reduce_scatter | solution.py:394
  68.9 127.6 %copy-start.46 = (f32[14,14,64]{2,1,0:T(8,128)}, f32[14,14,64]{2,1,0:T(8,128)S(1)}, u32[]{:S(2)}) copy-start(f32[14,14,64]{2,1,0:T(8,128)S(1)} %fusion.193) | copy-start | bytes 150532
  69.0 19.1 %collective-permute-start.1 = (bf16[1,32,16,768]{3,2,1,0:T(8,128)(2,1)S(1)}, bf16[1,32,16,768]{3,2,1,0:T(8,128)(2,1)S(1)}, u32[]{:S(2)}, u32[]{:S(2)}) collective-permute-start(bf16[1,32,16,768]{3,2,1,0:T(8,128)(2,1)S(1)} %pad_maximum_fusion.7), channel_id=1, source_target_pairs={{1,0},{2,1},{3,2},{5,4},{6,5},{7,6},{9,8},{10,9},{11,10},{13,12},{... | collective-permute-start | bytes 2359304 | tf_op jit(solution)/shard_map/ppermute | solution.py:20
  70.5 135.4 %copy-start.66 = (f32[14,14,64]{2,1,0:T(8,128)}, f32[14,14,64]{2,1,0:T(8,128)S(1)}, u32[]{:S(2)}) copy-start(f32[14,14,64]{2,1,0:T(8,128)S(1)} %fusion.195) | copy-start | bytes 150532
  71.5 34.8 %collective-permute-start.5 = (bf16[1,32,16,768]{3,2,1,0:T(8,128)(2,1)}, bf16[1,32,16,768]{3,2,1,0:T(8,128)(2,1)}, u32[]{:S(2)}, u32[]{:S(2)}) collective-permute-start(bf16[1,32,16,768]{3,2,1,0:T(8,128)(2,1)} %pad_maximum_fusion.8), channel_id=1, source_target_pairs={{1,0},{2,1},{3,2},{5,4},{6,5},{7,6},{9,8},{10,9},{11,10},{13,12},{... | collective-permute-start | bytes 2359304 | tf_op jit(solution)/shard_map/ppermute | solution.py:20
  145.4 42.3 %copy-start.6 = (bf16[4,196,1,12,64]{4,0,3,1,2:T(4,128)(2,1)}, bf16[4,196,1,12,64]{4,0,3,1,2:T(4,128)(2,1)S(1)}, u32[]{:S(2)}) copy-start(bf16[4,196,1,12,64]{4,0,3,1,2:T(4,128)(2,1)S(1)} %copy.397) | copy-start | bytes 3612676
  178.8 27.2 %copy-start.4 = (bf16[4,196,1,12,64]{4,0,3,1,2:T(4,128)(2,1)}, bf16[4,196,1,12,64]{4,0,3,1,2:T(4,128)(2,1)S(1)}, u32[]{:S(2)}) copy-start(bf16[4,196,1,12,64]{4,0,3,1,2:T(4,128)(2,1)S(1)} %copy.411) | copy-start | bytes 3612676
  246.8 182.1 %copy-start.17 = (bf16[4,196,1,12,64]{1,4,3,0,2:T(8,128)(2,1)}, bf16[4,196,1,12,64]{1,4,3,0,2:T(8,128)(2,1)S(1)}, u32[]{:S(2)}) copy-start(bf16[4,196,1,12,64]{1,4,3,0,2:T(8,128)(2,1)S(1)} %copy.513) | copy-start | bytes 3612676
  479.8 31.2 %copy-start.27 = (bf16[1,32,32,768]{3,2,1,0:T(8,128)(2,1)}, bf16[1,32,32,768]{3,2,1,0:T(8,128)(2,1)S(1)}, u32[]{:S(2)}) copy-start(bf16[1,32,32,768]{3,2,1,0:T(8,128)(2,1)S(1)} %select_n.254) | copy-start | bytes 4718596
  480.8 224.1 %collective-permute-start.6 = (bf16[1,32,16,768]{3,2,1,0:T(8,128)(2,1)}, bf16[1,32,16,768]{3,2,1,0:T(8,128)(2,1)}, u32[]{:S(2)}, u32[]{:S(2)}) collective-permute-start(bf16[1,32,16,768]{3,2,1,0:T(8,128)(2,1)} %slice.231), channel_id=1, source_target_pairs={{0,1},{1,2},{2,3},{4,5},{5,6},{6,7},{8,9},{9,10},{10,11},{12,13},{... | collective-permute-start | bytes 2359304 | tf_op jit(solution)/shard_map/ppermute | solution.py:20
  683.3 20.3 %copy-start.10 = (bf16[2,1,16,16,768]{4,3,2,1,0:T(8,128)(2,1)S(1)}, bf16[2,1,16,16,768]{4,3,2,1,0:T(8,128)(2,1)}, u32[]{:S(2)}) copy-start(bf16[2,1,16,16,768]{4,3,2,1,0:T(8,128)(2,1)} %param.16) | copy-start | bytes 2359300
  702.1 18.2 %copy-start.30 = (bf16[1,32,32,768]{3,2,1,0:T(8,128)(2,1)S(1)}, bf16[1,32,32,768]{3,2,1,0:T(8,128)(2,1)}, u32[]{:S(2)}) copy-start(bf16[1,32,32,768]{3,2,1,0:T(8,128)(2,1)} %select_n.242) | copy-start | bytes 4718596
  702.1 18.2 %collective-permute-start.2 = (bf16[1,32,16,768]{3,2,1,0:T(8,128)(2,1)S(1)}, bf16[1,32,16,768]{3,2,1,0:T(8,128)(2,1)S(1)}, u32[]{:S(2)}, u32[]{:S(2)}) collective-permute-start(bf16[1,32,16,768]{3,2,1,0:T(8,128)(2,1)S(1)} %slice.220), channel_id=1, source_target_pairs={{0,1},{1,2},{2,3},{4,5},{5,6},{6,7},{8,9},{9,10},{10,11},{12,13},{... | collective-permute-start | bytes 2359304 | tf_op jit(solution)/shard_map/ppermute | solution.py:20
  706.2 18.3 %copy-start.63 = (f32[1,1,16,16,768]{4,3,2,1,0:T(8,128)S(1)}, f32[1,1,16,16,768]{4,3,2,1,0:T(8,128)}, u32[]{:S(2)}) copy-start(f32[1,1,16,16,768]{4,3,2,1,0:T(8,128)} %get-tuple-element.109) | copy-start | bytes 2359300
  706.3 18.3 %copy-start.104 = (f32[768]{0:T(1024)S(1)}, f32[768]{0:T(1024)}, u32[]{:S(2)}) copy-start(f32[768]{0:T(1024)} %convert_element_type.330) | copy-start | bytes 9220
  706.3 18.1 %collective-permute-start.7 = (bf16[1,16,16,768]{3,2,1,0:T(8,128)(2,1)S(1)}, bf16[1,16,16,768]{3,2,1,0:T(8,128)(2,1)S(1)}, u32[]{:S(2)}, u32[]{:S(2)}) collective-permute-start(bf16[1,16,16,768]{3,2,1,0:T(8,128)(2,1)S(1)} %slice.233), channel_id=1, source_target_pairs={{0,4},{4,8},{8,12},{1,5},{5,9},{9,13},{2,6},{6,10},{10,14},{3,7},{... | collective-permute-start | bytes 1179656 | tf_op jit(solution)/shard_map/ppermute | solution.py:20
  720.4 6.3 collective-permute-start.3
  726.5 40.4 %copy-start.13 = (f32[256,768]{1,0:T(8,128)}, f32[256,768]{1,0:T(8,128)S(1)}, u32[]{:S(2)}) copy-start(f32[256,768]{1,0:T(8,128)S(1)} %get-tuple-element.123) | copy-start | bytes 2359300
  726.5 40.4 %copy-start.105 = (f32[256]{0:T(256)}, f32[256]{0:T(256)S(1)}, u32[]{:S(2)}) copy-start(f32[256]{0:T(256)S(1)} %broadcast_multiply_fusion.10) | copy-start | bytes 3076
  730.3 34.1 %copy-start.39 = (f32[256,768]{1,0:T(8,128)}, f32[256,768]{1,0:T(8,128)S(1)}, u32[]{:S(2)}) copy-start(f32[256,768]{1,0:T(8,128)S(1)} %get-tuple-element.129) | copy-start | bytes 2359300
  730.3 34.0 %copy-start.108 = (f32[256]{0:T(256)}, f32[256]{0:T(256)S(1)}, u32[]{:S(2)}) copy-start(f32[256]{0:T(256)S(1)} %broadcast_multiply_fusion.11) | copy-start | bytes 3076
  768.4 8.2 collective-permute-start.12
  770.9 9.7 collective-permute-start.8
  776.7 16.3 %collective-permute-start.13 = (bf16[1,32,16,768]{3,2,1,0:T(8,128)(2,1)S(1)}, bf16[1,32,16,768]{3,2,1,0:T(8,128)(2,1)}, u32[]{:S(2)}, u32[]{:S(2)}) collective-permute-start(bf16[1,32,16,768]{3,2,1,0:T(8,128)(2,1)S(1)} %pad_maximum_fusion.11), channel_id=1, source_target_pairs={{1,0},{2,1},{3,2},{5,4},{6,5},{7,6},{9,8},{10,9},{11,10},{13,12},{... | collective-permute-start | bytes 2359304 | tf_op jit(solution)/shard_map/ppermute | solution.py:20
  780.5 588.1 %reduce-scatter.5.cloned.1.call-start = ((), (), s32[]{:S(2)}) async-start(), calls=%async_computation.8 | async-start | bytes 7299072 | tf_op jit(solution)/shard_map/reduce_scatter | solution.py:392
  781.6 66.8 %collective-permute-start.9 = (bf16[1,32,16,768]{3,2,1,0:T(8,128)(2,1)}, bf16[1,32,16,768]{3,2,1,0:T(8,128)(2,1)}, u32[]{:S(2)}, u32[]{:S(2)}) collective-permute-start(bf16[1,32,16,768]{3,2,1,0:T(8,128)(2,1)} %pad_maximum_fusion.10), channel_id=1, source_target_pairs={{1,0},{2,1},{3,2},{5,4},{6,5},{7,6},{9,8},{10,9},{11,10},{13,12},{... | collective-permute-start | bytes 2359304 | tf_op jit(solution)/shard_map/ppermute | solution.py:20
  853.2 16.0 %copy-start.52 = (bf16[1,196,12,64]{1,3,2,0:T(8,128)(2,1)}, bf16[1,196,12,64]{1,3,2,0:T(8,128)(2,1)S(1)}, u32[]{:S(2)}) copy-start(bf16[1,196,12,64]{1,3,2,0:T(8,128)(2,1)S(1)} %copy.426) | copy-start | bytes 903172
  975.4 66.7 %copy-start.47 = (f32[14,14,64]{2,1,0:T(8,128)S(1)}, f32[14,14,64]{2,1,0:T(8,128)}, u32[]{:S(2)}) copy-start(f32[14,14,64]{2,1,0:T(8,128)} %copy-done.46) | copy-start | bytes 150532
  1169.0 284.5 %reduce-scatter.9.cloned.1.call-start = ((), (), s32[]{:S(2)}) async-start(), calls=%async_computation.10 | async-start | bytes 9732096 | tf_op jit(solution)/shard_map/reduce_scatter | solution.py:400
  1177.6 418.1 %reduce-scatter.11.cloned.1.call-start = ((), (), s32[]{:S(2)}) async-start(), calls=%async_computation.11 | async-start | bytes 9732096 | tf_op jit(solution)/shard_map/reduce_scatter | solution.py:402
  1224.9 72.0 %collective-permute-start.14 = (bf16[1,32,16,768]{3,2,1,0:T(8,128)(2,1)}, bf16[1,32,16,768]{3,2,1,0:T(8,128)(2,1)}, u32[]{:S(2)}, u32[]{:S(2)}) collective-permute-start(bf16[1,32,16,768]{3,2,1,0:T(8,128)(2,1)} %slice.247), channel_id=1, source_target_pairs={{0,1},{1,2},{2,3},{4,5},{5,6},{6,7},{8,9},{9,10},{10,11},{12,13},{... | collective-permute-start | bytes 2359304 | tf_op jit(solution)/shard_map/ppermute | solution.py:20
  1243.8 21.3 %copy-start.5 = (bf16[4,196,1,12,64]{4,0,3,1,2:T(4,128)(2,1)S(1)}, bf16[4,196,1,12,64]{4,0,3,1,2:T(4,128)(2,1)}, u32[]{:S(2)}) copy-start(bf16[4,196,1,12,64]{4,0,3,1,2:T(4,128)(2,1)} %copy-done.4) | copy-start | bytes 3612676
  1262.8 48.9 %collective-permute-start.10 = (bf16[1,32,16,768]{3,2,1,0:T(8,128)(2,1)S(1)}, bf16[1,32,16,768]{3,2,1,0:T(8,128)(2,1)}, u32[]{:S(2)}, u32[]{:S(2)}) collective-permute-start(bf16[1,32,16,768]{3,2,1,0:T(8,128)(2,1)S(1)} %slice.239), channel_id=1, source_target_pairs={{0,1},{1,2},{2,3},{4,5},{5,6},{6,7},{8,9},{9,10},{10,11},{12,13},{... | collective-permute-start | bytes 2359304 | tf_op jit(solution)/shard_map/ppermute | solution.py:20
  1296.9 19.6 %copy-start.11 = (bf16[2,1,16,16,768]{4,3,2,1,0:T(8,128)(2,1)S(1)}, bf16[2,1,16,16,768]{4,3,2,1,0:T(8,128)(2,1)}, u32[]{:S(2)}) copy-start(bf16[2,1,16,16,768]{4,3,2,1,0:T(8,128)(2,1)} %param.16) | copy-start | bytes 2359300
  1296.9 19.6 %copy-start.101 = (f32[768]{0:T(1024)S(1)}, f32[768]{0:T(1024)}, u32[]{:S(2)}) copy-start(f32[768]{0:T(1024)} %copy-done.100) | copy-start | bytes 9220
  1298.3 68.4 %copy-start.26 = (f32[256,768]{1,0:T(8,128)S(1)}, f32[256,768]{1,0:T(8,128)}, u32[]{:S(2)}) copy-start(f32[256,768]{1,0:T(8,128)} %copy-done.25) | copy-start | bytes 2359300
  1298.3 68.4 %copy-start.38 = (f32[256,768]{1,0:T(8,128)S(1)}, f32[256,768]{1,0:T(8,128)}, u32[]{:S(2)}) copy-start(f32[256,768]{1,0:T(8,128)} %copy-done.37) | copy-start | bytes 2359300
  1298.3 17.4 %collective-permute-start.15 = (bf16[1,16,16,768]{3,2,1,0:T(8,128)(2,1)S(1)}, bf16[1,16,16,768]{3,2,1,0:T(8,128)(2,1)S(1)}, u32[]{:S(2)}, u32[]{:S(2)}) collective-permute-start(bf16[1,16,16,768]{3,2,1,0:T(8,128)(2,1)S(1)} %slice.249), channel_id=1, source_target_pairs={{0,4},{4,8},{8,12},{1,5},{5,9},{9,13},{2,6},{6,10},{10,14},{3,7},{... | collective-permute-start | bytes 1179656 | tf_op jit(solution)/shard_map/ppermute | solution.py:20
  1313.2 3.3 collective-permute-start.11
  1366.7 229.0 %copy-start.1 = (bf16[27,64]{1,0:T(8,128)(2,1)S(1)}, bf16[27,64]{1,0:T(8,128)(2,1)}, u32[]{:S(2)}) copy-start(bf16[27,64]{1,0:T(8,128)(2,1)} %param.30) | copy-start | bytes 10372
  (111 other events, 651.4 us)
Sparse Core Ops, SparseCore 0:
  10.9 62.9 all-gather.4
  76.9 53.4 all-gather.6
  133.2 62.5 all-gather.8
  198.6 62.4 all-gather.10
  780.6 106.2 reduce-scatter.6
  1169.1 143.0 reduce-scatter.4
  1318.6 134.8 reduce-scatter.8
  1461.0 134.6 reduce-scatter.10
where the time goes:
time: 1620 us; the launch traced here: 1600 us
  local copies, waits for them, and re-layouts  751 us (46%)
  waiting for transfers between devices  283 us (17%)
  matrix products  274 us (17%)
  other arithmetic  147 us (9%)
  blocking collectives  87.2 us (5%)
  starting transfers between devices  42.7 us (3%)
  between operations  16.7 us (1%)
    add x12, local copies, waits for them, and re-layouts, window_scores(): scores.reshape(window_count, heads_here, WIN, WIN, WIN, WIN)  331 us
    reduce_scatter x1, waiting for transfers between devices, reduce_grads(): lax.psum_scatter(grad_down, ('dp', 'row', 'col'), scatter_dimension=0, ti...  142 us
    convert_element_type x4, local copies, waits for them, and re-layouts, attention_back(): row_sums = jnp.sum(split_grad, axis=5, dtype=jnp.float32)  103 us
    unnamed x2, blocking collectives  87.2 us
    reduce_scatter x1, waiting for transfers between devices, reduce_grads(): lax.psum_scatter(grad_up, ('dp', 'row', 'col'), scatter_dimension=0, tile...  85 us
    select_n x16, local copies, waits for them, and re-layouts, place_windows(): buffer = jnp.where(usable, updated, buffer)  79.4 us
    reduce_sum x1, other arithmetic, attention_back(): row_sums = jnp.sum(split_grad, axis=5, dtype=jnp.float32)  66.7 us
    ppermute x16, waiting for transfers between devices, shifted(): lax.ppermute(value, axis, [(source, source + steps) for source in range(f...  54 us
  transfers between devices with their start and end apart: 24, of which 8 were waited for; matrix products, arithmetic and copies ran while one was open for 71% of the time, Pallas kernels for 0%

commit v1 on v0

v1 whole, which is shorter than its diff:
```python
import math

import jax
import jax.numpy as jnp
import numpy as np
from jax import lax
from jax.experimental import pallas as pl
from jax.experimental.pallas import tpu as pltpu
from jax.sharding import PartitionSpec as P

HEAD = 64
WIN = 14
GRID = 64
NWIN = 5
PITCH = 16
KEYS = WIN * PITCH
LANES = 128
ROWFIELD, COLFIELD, LOWFIELD, MASKLANE = 0, 14, 28, 56
COLTABLE = 32
NEG = -1e30
EDGE = GRID - WIN * (NWIN - 1)
epsilon = 1e-06
bf16 = jnp.bfloat16
f32 = jnp.float32


def dot_nn(a, b):
    return lax.dot_general(a, b, (((1,), (0,)), ((), ())), preferred_element_type=f32)


def dot_nt(a, b):
    return lax.dot_general(a, b, (((1,), (1,)), ((), ())), preferred_element_type=f32)


def dot_tn(a, b):
    return lax.dot_general(a, b, (((0,), (0,)), ((), ())), preferred_element_type=f32)


def key_fields():
    ahead = np.zeros((KEYS, HEAD), np.float32)
    back = np.zeros((KEYS, HEAD), np.float32)
    for a in range(WIN):
        for b in range(PITCH):
            t = PITCH * a + b
            if b < WIN:
                for low in (0, LOWFIELD):
                    ahead[t, low + ROWFIELD + a] = 1
                    ahead[t, low + COLFIELD + b] = 1
                back[t, ROWFIELD + WIN - 1 - a] = 1
                back[t, COLFIELD + WIN - 1 - b] = 1
            else:
                ahead[t, MASKLANE] = NEG
    both = lambda x: jnp.asarray(np.concatenate([x, x], 1), bf16)
    return both(ahead), both(back)


def table_matrix(row_tab, col_tab, reverse):
    half = jnp.zeros((HEAD, HEAD), bf16)
    a, b = (row_tab[::-1], col_tab[::-1]) if reverse else (row_tab, col_tab)
    half = half.at[:, : 2 * WIN - 1].set(a.T).at[:, COLTABLE : COLTABLE + 2 * WIN - 1].set(b.T)
    none = jnp.zeros_like(half)
    return jnp.concatenate(
        [jnp.concatenate([none, half], 1), jnp.concatenate([half, none], 1)], 0
    )


def lane_in(shape, start, count):
    lane = lax.broadcasted_iota(jnp.int32, shape, 1) % HEAD
    return (lane >= start) & (lane < start + count)


def query_fields(q2, table):
    turned = dot_nn(q2, table)
    parts = []
    shape = (PITCH, LANES)
    in_rows = lane_in(shape, ROWFIELD, WIN)
    in_cols = lane_in(shape, COLFIELD, WIN)
    for a in range(q2.shape[0] // PITCH):
        t = turned[PITCH * a : PITCH * (a + 1)]
        r = pltpu.roll(t, (a - WIN + 1) % LANES, 1)
        c = pltpu.roll(t, LANES - (COLTABLE + 2 * WIN - 2 - (WIN - 1) - COLFIELD), 1, stride=1, stride_axis=0)
        parts.append(jnp.where(in_rows, r, jnp.where(in_cols, c, 0.0)))
    full = jnp.concatenate(parts, 0)
    high = full.astype(bf16).astype(f32)
    low = pltpu.roll(full - high, LOWFIELD, 1)
    one = jnp.where(lane_in(full.shape, MASKLANE, 1), 1.0, 0.0)
    return (high + low + one).astype(bf16)


def field_tables(fields):
    parts = []
    shape = (PITCH, LANES)
    in_rows = lane_in(shape, ROWFIELD, WIN)
    in_cols = lane_in(shape, COLFIELD, WIN)
    for a in range(fields.shape[0] // PITCH):
        t = fields[PITCH * a : PITCH * (a + 1)]
        r = jnp.where(in_rows, t, 0.0)
        c = jnp.where(in_cols, t, 0.0)
        r = pltpu.roll(r, a, 1) if a else r
        c = pltpu.roll(c, COLTABLE - COLFIELD, 1, stride=1, stride_axis=0)
        parts.append(r + c)
    return jnp.concatenate(parts, 0)


def first_half(shape, axis):
    return lax.broadcasted_iota(jnp.int32, shape, axis) < HEAD


def padded_rows(block, fill):
    if block.shape[0] == KEYS:
        return block
    rest = (KEYS - block.shape[0], LANES)
    return jnp.concatenate([block, jnp.broadcast_to(fill, rest).astype(block.dtype)], 0)


def attend_kernel(slots, q_ref, k_ref, v_ref, vb_ref, tab_ref, kf_ref, att_ref, lse_ref):
    kf = kf_ref[...]
    for s, (row, count, lane0) in enumerate(slots):
        rows = pl.ds(row, count)
        q2 = q_ref[rows, :]
        k2 = padded_rows(k_ref[rows, :] * bf16(HEAD ** -0.5), jnp.zeros((1, LANES), bf16))
        v2 = padded_rows(v_ref[rows, :], vb_ref[0:1, :])
        x2 = query_fields(q2, tab_ref[s])
        left = first_half((count, LANES), 1)
        leftk = first_half((KEYS, LANES), 1)
        outs = []
        for e in range(2):
            qa = jnp.where(left, q2, x2) if e == 0 else jnp.where(left, x2, q2)
            ka = jnp.where(leftk, k2, kf) if e == 0 else jnp.where(leftk, kf, k2)
            one = jnp.ones((KEYS, LANES), bf16)
            va = jnp.where(leftk, v2, one) if e == 0 else jnp.where(leftk, one, v2)
            st = dot_nt(ka, qa)
            peak = jnp.max(st, axis=0, keepdims=True)
            pt = jnp.exp(st - peak).astype(bf16)
            ot = dot_tn(va, pt)
            mass = ot[HEAD : HEAD + 1] if e == 0 else ot[0:1]
            lse_ref[0, e : e + 1, lane0 : lane0 + count] = peak + jnp.log(mass)
            outs.append(ot * (1.0 / mass))
        both = jnp.where(first_half((LANES, count), 0), outs[0], outs[1])
        att_ref[rows, :] = both.T.astype(bf16)


def attend_back_kernel(
    slots, q_ref, k_ref, v_ref, do_ref, lse_ref, vb_ref, tab_ref, tabb_ref, kf_ref, kb_ref,
    dqkv_ref, dtab_ref, dvb_ref,
):
    kf = kf_ref[...]
    kb = kb_ref[...]
    extra = jnp.zeros((1, LANES), f32)

    @pl.when(pl.program_id(0) == 0)
    def _():
        dtab_ref[...] = jnp.zeros_like(dtab_ref)

    for s, (row, count, lane0) in enumerate(slots):
        rows = pl.ds(row, count)
        q2 = q_ref[rows, :]
        do2 = do_ref[rows, :]
        k2 = padded_rows(k_ref[rows, :] * bf16(HEAD ** -0.5), jnp.zeros((1, LANES), bf16))
        v2 = padded_rows(v_ref[rows, :], vb_ref[0:1, :])
        x2 = query_fields(q2, tab_ref[s])
        left = first_half((count, LANES), 1)
        leftk = first_half((KEYS, LANES), 1)
        zero = jnp.zeros((KEYS, LANES), bf16)
        dq, dk, dv = [], [], []
        for e in range(2):
            qa = jnp.where(left, q2, x2) if e == 0 else jnp.where(left, x2, q2)
            ka = jnp.where(leftk, k2, kf) if e == 0 else jnp.where(leftk, kf, k2)
            kr = jnp.where(leftk, k2, kb) if e == 0 else jnp.where(leftk, kb, k2)
            va = jnp.where(leftk, v2, zero) if e == 0 else jnp.where(leftk, zero, v2)
            st = dot_nt(ka, qa)
            pt = jnp.exp(st - lse_ref[0, e : e + 1, lane0 : lane0 + count])
            dpt = dot_nt(va, do2)
            mean = jnp.sum(pt * dpt, axis=0, keepdims=True)
            dst = (pt * (dpt - mean)).astype(bf16)
            dv.append(dot_nn(pt.astype(bf16), do2))
            dk.append(dot_nn(dst, qa))
            dq.append(dot_tn(dst, kr))
        fields = jnp.where(left, dq[1], dq[0])
        dt = field_tables(fields)
        high = dt.astype(bf16)
        low = (dt - high.astype(f32)).astype(bf16)
        tabb = tabb_ref[s]
        dq2 = jnp.where(left, dq[0], dq[1]) + dot_nt(high, tabb) + dot_nt(low, tabb)
        dk2 = jnp.where(leftk, dk[0], dk[1]) * (HEAD ** -0.5)
        dv2 = jnp.where(leftk, dv[0], dv[1])
        dqkv_ref[0, rows, :] = dq2.astype(bf16)
        dqkv_ref[1, rows, :] = dk2[:count].astype(bf16)
        dqkv_ref[2, rows, :] = dv2[:count].astype(bf16)
        if count < KEYS:
            extra = extra + jnp.sum(dv2[count:], axis=0, keepdims=True)
        dtab_ref[s] += dot_tn(q2, high) + dot_tn(q2, low)
    dvb_ref[0] = jnp.broadcast_to(extra, (8, LANES))


def slot_places(counts):
    places, row, lane = [], 0, 0
    for count in counts:
        places.append((row, count, lane))
        row += count
        lane += -(-count // LANES) * LANES
    return tuple(places), row, lane


def attend(projected, bias_v, tables, counts):
    slots, rows, lanes = slot_places(counts)
    width = projected.shape[1] // 3
    pairs = width // LANES
    kf, _ = key_fields()
    col = lambda off: pl.BlockSpec((rows, LANES), lambda p: (0, off * pairs + p))
    return pl.pallas_call(
        lambda *refs: attend_kernel(slots, *refs),
        grid=(pairs,),
        in_specs=[
            col(0), col(1), col(2),
            pl.BlockSpec((8, LANES), lambda p: (0, p)),
            pl.BlockSpec((len(counts), LANES, LANES), lambda p: (0, 0, 0)),
            pl.BlockSpec((KEYS, LANES), lambda p: (0, 0)),
        ],
        out_specs=[
            pl.BlockSpec((rows, LANES), lambda p: (0, p)),
            pl.BlockSpec((1, 8, lanes), lambda p: (p, 0, 0)),
        ],
        out_shape=[
            jax.ShapeDtypeStruct((rows, width), bf16),
            jax.ShapeDtypeStruct((pairs, 8, lanes), f32),
        ],
        compiler_params=pltpu.CompilerParams(vmem_limit_bytes=48 << 20),
        name="attend",
    )(projected, projected, projected, bias_v, tables, kf)


def attend_back(projected, upstream, lse, bias_v, tables, tables_back, counts):
    slots, rows, lanes = slot_places(counts)
    width = projected.shape[1] // 3
    pairs = width // LANES
    kf, kb = key_fields()
    col = lambda off: pl.BlockSpec((rows, LANES), lambda p: (0, off * pairs + p))
    n = len(counts)
    return pl.pallas_call(
        lambda *refs: attend_back_kernel(slots, *refs),
        grid=(pairs,),
        in_specs=[
            col(0), col(1), col(2), col(0),
            pl.BlockSpec((1, 8, lanes), lambda p: (p, 0, 0)),
            pl.BlockSpec((8, LANES), lambda p: (0, p)),
            pl.BlockSpec((n, LANES, LANES), lambda p: (0, 0, 0)),
            pl.BlockSpec((n, LANES, LANES), lambda p: (0, 0, 0)),
            pl.BlockSpec((KEYS, LANES), lambda p: (0, 0)),
            pl.BlockSpec((KEYS, LANES), lambda p: (0, 0)),
        ],
        out_specs=[
            pl.BlockSpec((3, rows, LANES), lambda p: (0, 0, p)),
            pl.BlockSpec((n, LANES, LANES), lambda p: (0, 0, 0)),
            pl.BlockSpec((1, 8, LANES), lambda p: (p, 0, 0)),
        ],
        out_shape=[
            jax.ShapeDtypeStruct((3, rows, width), bf16),
            jax.ShapeDtypeStruct((n, LANES, LANES), f32),
            jax.ShapeDtypeStruct((pairs, 8, LANES), f32),
        ],
        compiler_params=pltpu.CompilerParams(vmem_limit_bytes=48 << 20),
        name="attend_back",
    )(projected, projected, projected, upstream, lse, bias_v, tables, tables_back, kf, kb)


def sides(index):
    return WIN * index, min(WIN * index + WIN, GRID)


class Plan:
    def __init__(self, rows, cols, images):
        self.rows, self.cols, self.images = rows, cols, images
        self.devices = rows * cols
        self.tile_rows, self.tile_cols = GRID // rows, GRID // cols
        self.tokens = images * self.tile_rows * self.tile_cols
        kinds = ([], [], [])
        for n in range(images):
            for i in range(NWIN):
                for j in range(NWIN):
                    kinds[(i == NWIN - 1) + (j == NWIN - 1)].append((n, i, j))
        self.caps = tuple(-(-len(kind) // self.devices) for kind in kinds)
        self.parts = {w: self._sources(w) for kind in kinds for w in kind}
        owner = self._assign(kinds)
        self.counts = (KEYS,) * self.caps[0] + (EDGE * PITCH,) * (self.caps[1] + self.caps[2])
        _, self.window_rows, _ = slot_places(self.counts)
        self._tables(kinds, owner)

    def _distance(self, one, two):
        r, c = divmod(one, self.cols)
        q, e = divmod(two, self.cols)
        return abs(c - e) + abs(r // 2 - q // 2) + (0.125 if r % 2 != q % 2 else 0.0)

    def _sources(self, window):
        _, i, j = window
        (r0, r1), (c0, c1) = sides(i), sides(j)
        tr, tc = self.tile_rows, self.tile_cols
        found = {}
        for r in range(r0 // tr, (r1 - 1) // tr + 1):
            for c in range(c0 // tc, (c1 - 1) // tc + 1):
                high = min(r1, (r + 1) * tr) - max(r0, r * tr)
                wide = min(c1, (c + 1) * tc) - max(c0, c * tc)
                found[r * self.cols + c] = high * wide
        return found

    def _rounds(self, owner):
        pairs = {}
        for window, dev in owner.items():
            for source, amount in self.parts[window].items():
                if source != dev:
                    pairs[source, dev] = pairs.get((source, dev), 0) + amount
        rounds = []
        for pair, amount in sorted(pairs.items(), key=lambda p: (-p[1], p[0])):
            for senders, takers, members in rounds:
                if pair[0] not in senders and pair[1] not in takers:
                    break
            else:
                senders, takers, members = set(), set(), []
                rounds.append((senders, takers, members))
            senders.add(pair[0])
            takers.add(pair[1])
            members.append(pair)
        return pairs, [members for _, _, members in rounds]

    def _cost(self, owner):
        pairs, rounds = self._rounds(owner)
        moved = sum(amount * self._distance(*pair) for pair, amount in pairs.items())
        return moved / 4 + sum(64 + max(pairs[p] for p in members) for members in rounds)

    def _assign(self, kinds):
        owner = {}
        room = {}
        for kind, windows in enumerate(kinds):
            room[kind] = [self.caps[kind]] * self.devices
            for window in sorted(windows, key=lambda w: (-(w[1] + w[2]), w)):
                far = lambda d: sum(t * self._distance(s, d) for s, t in self.parts[window].items())
                dev = min((d for d in range(self.devices) if room[kind][d]), key=lambda d: (far(d), d))
                owner[window] = dev
                room[kind][dev] -= 1
        best = self._cost(owner)
        for _ in range(4):
            before = best
            for kind in (1, 2, 0):
                for one in kinds[kind]:
                    for dev in range(self.devices):
                        if dev == owner[one]:
                            continue
                        trials = []
                        if room[kind][dev]:
                            trials.append({**owner, one: dev})
                        for two in kinds[kind]:
                            if owner[two] == dev:
                                trials.append({**owner, one: dev, two: owner[one]})
                        for trial in trials:
                            price = self._cost(trial)
                            if price < best - 1e-9:
                                if sum(trial[w] != owner[w] for w in kinds[kind]) == 1:
                                    room[kind][owner[one]] += 1
                                    room[kind][dev] -= 1
                                owner, best = trial, price
                                break
            if best >= before:
                break
        return owner

    def _tables(self, kinds, owner):
        places, _, _ = slot_places(self.counts)
        starts = (0, self.caps[0], self.caps[0] + self.caps[1])
        self.swapped = np.zeros((self.devices, len(self.counts)), np.int32)
        taken = {}
        moves = {}
        for kind, windows in enumerate(kinds):
            for window in windows:
                n, i, j = window
                dev = owner[window]
                slot = starts[kind] + taken.get((dev, kind), 0)
                taken[dev, kind] = taken.get((dev, kind), 0) + 1
                swap = kind == 1 and j == NWIN - 1
                self.swapped[dev, slot] = swap
                (r0, r1), (c0, c1) = sides(i), sides(j)
                for r in range(r0, r1):
                    for c in range(c0, c1):
                        a, b = (c - c0, r - r0) if swap else (r - r0, c - c0)
                        row = places[slot][0] + PITCH * a + b
                        source = (r // self.tile_rows) * self.cols + c // self.tile_cols
                        token = (n * self.tile_rows + r % self.tile_rows) * self.tile_cols
                        token += c % self.tile_cols
                        moves.setdefault((source, dev), []).append((token, row))
        _, rounds = self._rounds(owner)
        self.perms = rounds
        self.sizes = [-(-max(len(moves[p]) for p in members) // PITCH) * PITCH for members in rounds]
        total = sum(self.sizes)
        self.pack = np.full((self.devices, total), -1, np.int32)
        self.take = np.full((self.devices, self.window_rows), -1, np.int32)
        self.pack_back = np.full((self.devices, total), -1, np.int32)
        self.take_back = np.full((self.devices, self.tokens), -1, np.int32)
        for dev in range(self.devices):
            for token, row in moves.get((dev, dev), ()):
                self.take[dev, row] = token
                self.take_back[dev, token] = row
        at = 0
        for members, size in zip(rounds, self.sizes):
            for source, dev in members:
                for k, (token, row) in enumerate(moves[source, dev]):
                    self.pack[source, at + k] = token
                    self.take[dev, row] = self.tokens + at + k
                    self.pack_back[dev, at + k] = row
                    self.take_back[source, token] = self.window_rows + at + k
            at += size


def chosen(index, start, count):
    spot = lax.broadcasted_iota(jnp.int32, (count, index.shape[1]), 0) + start
    return jnp.where(spot == index, 1.0, 0.0).astype(bf16)


def pack_kernel(sizes, index_ref, tokens_ref, *out_refs):
    at = 0
    tokens = tokens_ref[...].astype(bf16)
    for size, out_ref in zip(sizes, out_refs):
        index = index_ref[0:1, at : at + size]
        out_ref[...] = dot_tn(chosen(index, 0, tokens.shape[0]), tokens).astype(bf16)
        at += size


def pack(index, tokens, sizes):
    return pl.pallas_call(
        lambda *refs: pack_kernel(sizes, *refs),
        out_shape=[jax.ShapeDtypeStruct((size, tokens.shape[1]), bf16) for size in sizes],
        compiler_params=pltpu.CompilerParams(vmem_limit_bytes=40 << 20),
        name="pack",
    )(index[None], tokens)


def take_kernel(index_ref, local_ref, *refs):
    out_ref = refs[-1]
    index = index_ref[...]
    local = local_ref[...]
    hot = chosen(index, 0, local.shape[0])
    total = dot_tn(hot, local.astype(bf16))
    if local.dtype == f32:
        total = total + dot_tn(hot, (local - local.astype(bf16).astype(f32)).astype(bf16))
    at = local.shape[0]
    for ref in refs[:-1]:
        total = total + dot_tn(chosen(index, at, ref.shape[0]), ref[...])
        at += ref.shape[0]
    out_ref[...] = total.astype(out_ref.dtype)


def take(index, local, arrived):
    return pl.pallas_call(
        take_kernel,
        out_shape=jax.ShapeDtypeStruct((index.shape[0], local.shape[1]), local.dtype),
        compiler_params=pltpu.CompilerParams(vmem_limit_bytes=40 << 20),
        name="take",
    )(index[None], local, *arrived)


class Mover:
    def __init__(self, plan):
        self.plan = plan
        here = lax.axis_index("row") * plan.cols + lax.axis_index("col")
        mine = lambda table: lax.dynamic_index_in_dim(jnp.asarray(table), here, 0, keepdims=False)
        self.index = {name: mine(getattr(plan, name)) for name in ("pack", "take", "pack_back", "take_back")}
        self.swapped = mine(plan.swapped)

    def to_windows(self, tokens):
        sent = pack(self.index["pack"], tokens, self.plan.sizes)
        arrived = [lax.ppermute(s, ("row", "col"), perm) for s, perm in zip(sent, self.plan.perms)]
        return take(self.index["take"], tokens, arrived)

    def to_tile(self, rows):
        sent = pack(self.index["pack_back"], rows, self.plan.sizes)
        arrived = [
            lax.ppermute(s, ("row", "col"), [(d, s2) for s2, d in perm])
            for s, perm in zip(sent, self.plan.perms)
        ]
        return take(self.index["take_back"], rows, arrived)


AXES = ("dp", "row", "col")
TORUS = (2, 4, 4)


def over_dp(v):
    return lax.ppermute(v, "dp", [(0, 1), (1, 0)])


def over_y(v):
    return lax.ppermute(v, "row", [(r, (r + 2) % 4) for r in range(4)])


def over_core(v):
    return lax.ppermute(v, "row", [(r, r ^ 1) for r in range(4)])


def over_col(v, steps):
    return lax.ppermute(v, "col", [(c, (c + steps) % 4) for c in range(4)])


def block_at(flip_dp, flip_y, flip_core):
    dp, row = lax.axis_index("dp"), lax.axis_index("row")
    return (
        ((dp + flip_dp) % 2) * 4 + ((row // 2 + flip_y) % 2) * 2 + (row % 2 + flip_core) % 2
    )


def gather_pieces(shard):
    place = lax.axis_index("col")
    seen = [shard] + [over_col(shard, k) for k in (1, 2, 3)]
    column = []
    for j in range(4):
        block = seen[0]
        for k in (1, 2, 3):
            block = jnp.where((place - j) % 4 == k, seen[k], block)
        column.append(block)
    own = jnp.concatenate(column, 0)
    half = shard.shape[1] // 2
    by_dp, by_y = over_dp(own), over_y(own)
    diag_low, diag_high = over_dp(by_y[:, :half]), over_y(by_dp[:, half:])
    pieces = [own, by_dp, by_y, diag_low, diag_high]
    return pieces + [over_core(p) for p in pieces]


def place_kernel(half, *refs):
    pieces, out_ref, sems = refs[:10], refs[10], refs[11]
    copies = []
    for k, piece in enumerate(pieces):
        core, kind = divmod(k, 5)
        block = block_at(kind in (1, 3, 4), kind in (2, 3, 4), core)
        target = out_ref.at[block]
        if kind == 3:
            target = out_ref.at[block, :, pl.ds(0, half)]
        if kind == 4:
            target = out_ref.at[block, :, pl.ds(half, half)]
        copies.append(pltpu.make_async_copy(piece, target, sems.at[k]))
    for copy in copies:
        copy.start()
    for copy in copies:
        copy.wait()


def gather_rows(shard):
    pieces = gather_pieces(shard)
    rows, width = pieces[0].shape
    whole = pl.pallas_call(
        lambda *refs: place_kernel(width // 2, *refs),
        out_specs=pl.BlockSpec(memory_space=pl.ANY),
        out_shape=jax.ShapeDtypeStruct((8, rows, width), shard.dtype),
        scratch_shapes=[pltpu.SemaphoreType.DMA((10,))],
        compiler_params=pltpu.CompilerParams(vmem_limit_bytes=40 << 20),
        name="place",
    )(*pieces)
    return whole.reshape(8 * rows, width)


def scatter_sum(grad):
    rows, width = grad.shape[0] // 8, grad.shape[1]
    half = width // 2
    blocks = grad.reshape(8, rows, width)
    kinds = ((0, 0), (1, 0), (0, 1), (1, 1))
    pick = lambda kind, core: lax.dynamic_index_in_dim(blocks, block_at(*kind, core), 0, False)
    other = over_core(jnp.stack([pick(kind, 1) for kind in kinds]))
    own, to_dp, to_y, diag = [
        pick(kind, 0).astype(f32) + other[k].astype(f32) for k, kind in enumerate(kinds)
    ]
    diag = diag.astype(bf16)
    low, high = over_dp(diag[:, :half]), over_y(diag[:, half:])
    to_dp = jnp.concatenate([to_dp[:, :half], to_dp[:, half:] + high.astype(f32)], 1).astype(bf16)
    to_y = jnp.concatenate([to_y[:, :half] + low.astype(f32), to_y[:, half:]], 1).astype(bf16)
    column = own + over_dp(to_dp).astype(f32) + over_y(to_y).astype(f32)
    column = column.reshape(4, rows // 4, width)
    sent = column.astype(bf16)
    place = lax.axis_index("col")
    total = lax.dynamic_index_in_dim(column, place, 0, False)
    for k in (1, 2, 3):
        step = over_col(lax.dynamic_index_in_dim(sent, (place + k) % 4, 0, False), k)
        total = total + step.astype(f32)
    return total


def tree_sum(value):
    value = value + over_col(value, 1) + over_col(value, 2) + over_col(value, 3)
    value = value + over_dp(value)
    value = value + over_y(value)
    return value + over_core(value)


def on_torus():
    return tuple(lax.axis_size(a) for a in AXES) == TORUS


def device_number():
    return (lax.axis_index("dp") * lax.axis_size("row") + lax.axis_index("row")) * lax.axis_size(
        "col"
    ) + lax.axis_index("col")


def whole_weight(shard):
    if on_torus():
        return gather_rows(shard)
    return lax.all_gather(shard, AXES, axis=0, tiled=True)


def shared_sum(grad):
    if on_torus():
        return scatter_sum(grad.astype(bf16))
    return lax.psum_scatter(grad, AXES, scatter_dimension=0, tiled=True)


def sum_everywhere(value):
    if on_torus():
        return tree_sum(value)
    return lax.psum(value, AXES)


def whole_vectors(shards):
    count = lax.axis_size("dp") * lax.axis_size("row") * lax.axis_size("col")
    packed = jnp.concatenate(shards)
    spot = lax.broadcasted_iota(jnp.int32, (count, packed.shape[0]), 0) == device_number()
    table = sum_everywhere(jnp.where(spot, packed[None], jnp.zeros((), bf16)))
    vectors, at = [], 0
    for shard in shards:
        vectors.append(table[:, at : at + shard.shape[0]].reshape(-1))
        at += shard.shape[0]
    return vectors


def shared_vectors(vectors, tables):
    count = lax.axis_size("dp") * lax.axis_size("row") * lax.axis_size("col")
    flat = jnp.concatenate([v.reshape(-1) for v in (*vectors, *tables)])
    total = sum_everywhere(flat)
    mine, at = [], 0
    for vector in vectors:
        share = vector.shape[0] // count
        mine.append(lax.dynamic_slice(total, (at + device_number() * share,), (share,)))
        at += vector.shape[0]
    full = []
    for table in tables:
        full.append(total[at : at + table.size].reshape(table.shape))
        at += table.size
    return mine, full


def normalize(values):
    center = values - jnp.mean(values, axis=-1, keepdims=True)
    inverse = lax.rsqrt(jnp.mean(center * center, axis=-1, keepdims=True) + epsilon)
    return center * inverse, inverse


def norm_back(upstream, normed, inverse, gain):
    scaled = upstream * gain
    inner = jnp.mean(scaled, axis=-1, keepdims=True)
    cross = jnp.mean(scaled * normed, axis=-1, keepdims=True)
    result = inverse * (scaled - inner - normed * cross)
    return result, jnp.sum(upstream * normed, axis=0), jnp.sum(upstream, axis=0)


def body(
    images, qkv_weight, qv_bias, proj_weight, proj_bias, pre_gain, pre_shift, mid_gain, mid_shift,
    up_weight, up_bias, down_weight, down_bias, rel_rows, rel_cols, cotangent,
):
    width = images.shape[-1]
    plan = plan_for(lax.axis_size("row"), lax.axis_size("col"), images.shape[0] * images.shape[1])
    move = Mover(plan)
    counts = plan.counts
    x_low = move.to_windows(images.reshape(-1, width))
    qkv = whole_weight(qkv_weight)
    vectors = whole_vectors(
        [qv_bias, proj_bias, pre_gain, pre_shift, mid_gain, mid_shift, up_bias, down_bias]
    )
    qv, proj_add, gain_one, shift_one, gain_two, shift_two, up_add, down_add = [
        v.astype(f32) for v in vectors
    ]
    upstream = move.to_windows(cotangent.reshape(-1, width))
    proj = whole_weight(proj_weight)
    up = whole_weight(up_weight)
    down = whole_weight(down_weight)

    swapped = move.swapped[:, None, None] > 0
    ahead = [table_matrix(rel_rows, rel_cols, True), table_matrix(rel_cols, rel_rows, True)]
    back = [table_matrix(rel_rows, rel_cols, False), table_matrix(rel_cols, rel_rows, False)]
    tables = jnp.where(swapped, ahead[1][None], ahead[0][None])
    tables_back = jnp.where(swapped, back[1][None], back[0][None])

    real = (move.index["take"] >= 0)[:, None]
    x = x_low.astype(f32)
    plain_one, inverse_one = normalize(x)
    hidden = jnp.where(real, plain_one * gain_one + shift_one, 0.0).astype(bf16)
    full_bias = jnp.concatenate([qv[:width], jnp.zeros((width,), f32), qv[width:]])
    projected = (jnp.dot(hidden, qkv, preferred_element_type=f32) + full_bias).astype(bf16)
    bias_v = jnp.broadcast_to(qv[None, width:], (8, width)).astype(bf16)
    attended, logsum = attend(projected, bias_v, tables, counts)
    middle = x + jnp.dot(attended, proj, preferred_element_type=f32) + proj_add
    plain_two, inverse_two = normalize(middle)
    second = (plain_two * gain_two + shift_two).astype(bf16)
    inner = jnp.dot(second, up, preferred_element_type=f32) + up_add
    cdf = 0.5 * (1.0 + lax.erf(inner * 2.0 ** (-0.5)))
    pdf = jnp.exp(-0.5 * inner * inner) * (2.0 * math.pi) ** (-0.5)
    active = (inner * cdf).astype(bf16)
    slope = cdf + inner * pdf
    result = middle + jnp.dot(active, down, preferred_element_type=f32) + down_add
    out = move.to_tile(result.astype(bf16))

    flow = upstream.astype(f32)
    down_grad = shared_sum(dot_tn(active, upstream))
    inner_grad = (dot_nt(upstream, down) * slope).astype(bf16)
    up_grad = shared_sum(dot_tn(second, inner_grad))
    second_grad = dot_nt(inner_grad, up)
    part, mid_gain_grad, mid_shift_grad = norm_back(second_grad, plain_two, inverse_two, gain_two)
    middle_grad = flow + part
    branch = middle_grad.astype(bf16)
    proj_grad = shared_sum(dot_tn(attended, branch))
    attended_grad = dot_nt(branch, proj).astype(bf16)
    pieces, table_grads, bias_v_grad = attend_back(
        projected, attended_grad, logsum, bias_v, tables, tables_back, counts
    )
    projected_grad = jnp.concatenate([pieces[0], pieces[1], pieces[2]], 1)
    qkv_grad = shared_sum(dot_tn(hidden, projected_grad))
    hidden_grad = dot_nt(projected_grad, qkv).astype(bf16).astype(f32)
    hidden_grad = jnp.where(real, hidden_grad, 0.0)
    part, pre_gain_grad, pre_shift_grad = norm_back(hidden_grad, plain_one, inverse_one, gain_one)
    images_grad = move.to_tile(middle_grad + part)

    sums = jnp.sum(projected_grad, axis=0, dtype=f32)
    qv_grad = jnp.concatenate(
        [sums[:width], sums[2 * width :] + bias_v_grad[:, 0].reshape(-1)]
    )
    row_part, col_part = table_sums(table_grads)
    swap = move.swapped[:, None, None] > 0
    rows_grad = jnp.sum(jnp.where(swap, col_part, row_part), axis=0)
    cols_grad = jnp.sum(jnp.where(swap, row_part, col_part), axis=0)
    mine, full = shared_vectors(
        [
            qv_grad,
            jnp.sum(branch, axis=0, dtype=f32),
            pre_gain_grad,
            pre_shift_grad,
            mid_gain_grad,
            mid_shift_grad,
            jnp.sum(inner_grad, axis=0, dtype=f32),
            jnp.sum(flow, axis=0),
        ],
        [rows_grad, cols_grad],
    )
    return (
        out.reshape(images.shape),
        images_grad.reshape(images.shape),
        qkv_grad,
        mine[0],
        proj_grad,
        mine[1],
        mine[2],
        mine[3],
        mine[4],
        mine[5],
        up_grad,
        mine[6],
        down_grad,
        mine[7],
        full[0],
        full[1],
    )


def table_sums(grads):
    count = 2 * WIN - 1
    left, right = grads[:, :HEAD, HEAD:], grads[:, HEAD:, :HEAD]
    both = jnp.swapaxes(left + right, 1, 2)
    return both[:, :count], both[:, COLTABLE : COLTABLE + count]


PLANS = {}


def plan_for(rows, cols, images):
    key = (rows, cols, images)
    if key not in PLANS:
        PLANS[key] = Plan(*key)
    return PLANS[key]


def solution(mesh):
    tokens = P(None, "dp", "row", "col", None)
    rows = P(AXES, None)
    vector = P(AXES)
    placed = (
        tokens, rows, vector, rows, vector, vector, vector, vector, vector,
        rows, vector, rows, vector, P(), P(), tokens,
    )
    given = (tokens, tokens, rows, vector, rows, vector, vector, vector, vector, vector,
             rows, vector, rows, vector, P(), P())
    return jax.shard_map(body, mesh=mesh, in_specs=placed, out_specs=given, check_vma=False)
```

time: 1620 us -> 459 us (0.28)
  local copies, waits for them, and re-layouts: 751 us -> 49.5 us
  matrix products: 274 us -> 58.9 us
  waiting for transfers between devices: 283 us -> 91 us
  other arithmetic: 147 us -> 33.5 us
  starting transfers between devices: 42.7 us -> 143 us
  blocking collectives: 87.2 us -> 0 us
  Pallas kernels: 0 us -> 73.1 us
    add x14 -> x0, local copies, waits for them, and re-layouts: 342 us -> none  [the longest x12 331 us: window_scores(): scores.reshape(window_count, heads_here, WIN, WIN, WIN, WIN)]
    reduce_scatter x4 -> x0, waiting for transfers between devices: 227 us -> none  [the longest x1 142 us: reduce_grads(): lax.psum_scatter(grad_down, ('dp', 'row', 'col'), scatter_dimension=0, ti...]
    dot_general x54 -> x12, matrix products: 274 us -> 58.9 us  [the longest x4 20.7 us: dot_tn(): lax.dot_general(a, b, (((0,), (0,)), ((), ())), preferred_element_type=f32)]
    convert_element_type x10 -> x7, local copies, waits for them, and re-layouts: 145 us -> 2.93 us  [body(): v.astype(f32)]
    ppermute x16 -> x112, starting transfers between devices: 41.9 us -> 143 us  [the longest x30 51.7 us: over_col(): return lax.ppermute(v, 'col', [(c, (c + steps) % 4) for c in range(4)])]
    unnamed x2 -> x0, blocking collectives: 87.2 us -> none
    select_n x16 -> x0, local copies, waits for them, and re-layouts: 79.4 us -> none  [place_windows(): buffer = jnp.where(usable, updated, buffer)]
    reduce_sum x12 -> x6, other arithmetic: 81 us -> 2.86 us  [the longest x1 1.15 us: body(): jnp.sum(branch, axis=0, dtype=f32)]
  transfers between devices with their start and end apart: 24 -> 112, of which waited for: 8 -> 30; matrix products, arithmetic and copies ran while one was open for 71% -> 17% of each run, Pallas kernels for 0% -> 9%
where the time goes in v1:
time: 459 us; the launch traced here: 452 us
  starting transfers between devices  143 us (31%)
  waiting for transfers between devices  91 us (20%)
  Pallas kernels  73.1 us (16%)
  matrix products  58.9 us (13%)
  local copies, waits for them, and re-layouts  49.5 us (11%)
  other arithmetic  33.5 us (7%)
    ppermute x30, starting transfers between devices, over_col(): return lax.ppermute(v, 'col', [(c, (c + steps) % 4) for c in range(4)])  51.7 us
    ppermute x18, waiting for transfers between devices, over_y(): return lax.ppermute(v, 'row', [(r, (r + 2) % 4) for r in range(4)])  34.2 us
    pallas_call x1, Pallas kernels, attend_back(): pl.pallas_call(lambda *refs: attend_back_kernel(slots, *refs), grid=(pair...  30 us
    ppermute x18, waiting for transfers between devices, over_dp(): return lax.ppermute(v, 'dp', [(0, 1), (1, 0)])  29.6 us
    ppermute x18, starting transfers between devices, over_y(): return lax.ppermute(v, 'row', [(r, (r + 2) % 4) for r in range(4)])  24 us
    ppermute x30, waiting for transfers between devices, over_col(): return lax.ppermute(v, 'col', [(c, (c + steps) % 4) for c in range(4)])  24 us
    ppermute x10, starting transfers between devices, to_windows(): lax.ppermute(s, ('row', 'col'), perm)  24 us
    ppermute x10, starting transfers between devices, to_tile(): lax.ppermute(s, ('row', 'col'), [(d, s2) for s2, d in perm])  21.6 us
  transfers between devices with their start and end apart: 112, of which 30 were waited for; matrix products, arithmetic and copies ran while one was open for 17% of the time, Pallas kernels for 9%

profile of v1, /device:TPU:0, one launch (start us, length us, event | category | flops | bytes accessed | tf_op | source)
XLA Modules:
  0.0 452.3 jit_solution(14275854320078529326)
XLA Ops:
  0.7 5.6 %concatenate.108 = bf16[288]{0:T(512)(128)(2,1)S(1)} concatenate(bf16[48]{0:T(256)(128)(2,1)} %param.42, bf16[24]{0:T(256)(128)(2,1)} %param.44, bf16[24]{0:T(256)(128)(2,1)} %param.45, bf16[24]{0:T(256)(128)(2,1)} %param.46, bf16[24]{0:T(256)(128)(2,1)} %param.47, bf16[24]{0:T(256)(128)(2,1)} %param.48, bf16[96]{0:T(256)(128)(2,1)} %param.50, bf16[24]{0:T(256)(128)(2,1)} %param.52), dimensions={0} | concatenate | bytes 1152 | tf_op jit(solution)/shard_map/concatenate | solution.py:619
  6.4 4.1 collective-permute-start.6
  13.5 2.9 collective-permute-start.23
  34.5 2.8 collective-permute-start.11
  39.9 2.9 collective-permute-done.9
  47.2 5.5 %collective-permute-start.4 = (bf16[32,768]{1,0:T(8,128)(2,1)S(1)}, bf16[32,768]{1,0:T(8,128)(2,1)S(1)}, u32[]{:S(2)}, u32[]{:S(2)}) collective-permute-start(bf16[32,768]{1,0:T(8,128)(2,1)S(1)} %get-tuple-element.141), channel_id=1, source_target_pairs={{13,10},{1,6},{12,9},{0,5},{29,26},{17,22},{28,25},{16,21}} | collective-permute-start | bytes 147464 | tf_op jit(solution)/shard_map/ppermute | solution.py:469
  55.9 5.4 %collective-permute-start.36 = (bf16[24,3072]{1,0:T(8,128)(2,1)}, bf16[24,3072]{1,0:T(8,128)(2,1)S(1)}, u32[]{:S(2)}, u32[]{:S(2)}) collective-permute-start(bf16[24,3072]{1,0:T(8,128)(2,1)} %param.49), channel_id=1, source_target_pairs={{0,2},{1,3},{2,0},{3,1},{4,6},{5,7},{6,4},{7,5},{8,10},{9,11},{10,... | collective-permute-start | bytes 442376 | tf_op jit(solution)/shard_map/ppermute | solution.py:498
  69.3 3.9 collective-permute-done.35
  75.4 6.2 %collective-permute-start.49 = (bf16[96,768]{1,0:T(8,128)(2,1)}, bf16[96,768]{1,0:T(8,128)(2,1)S(1)}, u32[]{:S(2)}, u32[]{:S(2)}) collective-permute-start(bf16[96,768]{1,0:T(8,128)(2,1)} %param.51), channel_id=1, source_target_pairs={{0,1},{1,2},{2,3},{3,0},{4,5},{5,6},{6,7},{7,4},{8,9},{9,10},{10,1... | collective-permute-start | bytes 442376 | tf_op jit(solution)/shard_map/ppermute | solution.py:498
  84.1 4.2 collective-permute-start.64
  93.9 7.7 %collective-permute-start = (bf16[176,768]{1,0:T(8,128)(2,1)}, bf16[176,768]{1,0:T(8,128)(2,1)S(1)}, u32[]{:S(2)}, u32[]{:S(2)}) collective-permute-start(bf16[176,768]{1,0:T(8,128)(2,1)} %get-tuple-element.137), channel_id=1, source_target_pairs={{2,3},{8,12},{6,7},{9,13},{11,15},{15,11},{10,14},{1,2},{3,0},{4,8... | collective-permute-start | bytes 811016 | tf_op jit(solution)/shard_map/ppermute | solution.py:469
  101.6 3.0 collective-permute-done.29.refs_4_
  129.8 4.2 collective-permute-done.50.refs_1_
  135.8 2.3 collective-permute-done.39.refs_2_
  138.1 8.5 %collective-permute-done.38.refs_1_ = bf16[96,3072]{1,0:T(8,128)(2,1)} collective-permute-done((bf16[96,3072]{1,0:T(8,128)(2,1)S(1)}, bf16[96,3072]{1,0:T(8,128)(2,1)}, u32[]{:S(2)}, u32[]{:S(2)}) %collective-permute-start.38) | collective-permute-done | bytes 589856 | tf_op jit(solution)/shard_map/ppermute | solution.py:486
  160.2 3.0 place.4
  163.2 3.4 add_convert_fusion.refs_0_.refs_1_.refs_2_
  166.6 18.3 %attend.1 = (bf16[704,768]{1,0:T(8,128)(2,1)S(1)}, f32[6,8,768]{2,1,0:T(8,128)S(1)}) custom-call(bf16[704,2304]{1,0:T(8,128)(2,1)S(1)} %add_convert_fusion.refs_0_.refs_1_.refs_2_, bf16[704,2304]{1,0:T(8,128)(2,1)S(1)} %add_convert_fusion.refs_0_.refs_1_.refs_2_, bf16[704,2304]{1,0:T(8,128)(2,1)S(1)} %add_convert_fusion.refs_0_.refs_1_.refs_2_, ...), custom_call_target="tpu_custom_call" | custom-call | tf_op jit(solution)/shard_map/attend/pallas_call | solution.py:211
  188.5 7.3 %collective-permute-done.53.refs_4_ = bf16[384,384]{1,0:T(8,128)(2,1)S(1)} collective-permute-done((bf16[384,384]{1,0:T(8,128)(2,1)S(1)}, bf16[384,384]{1,0:T(8,128)(2,1)S(1)}, u32[]{:S(2)}, u32[]{:S(2)}) %collective-permute-start.53) | collective-permute-done | bytes 294944 | tf_op jit(solution)/shard_map/ppermute | solution.py:490
  204.1 7.3 %multiply_convert_fusion = (bf16[704,3072]{1,0:T(8,128)(2,1)}, f32[704,3072]{1,0:T(8,128)}) fusion(f32[3072]{0:T(1024)S(1)} %reshape.482, bf16[768,3072]{1,0:T(8,128)(2,1)S(1)} %bitcast.156, f32[704,768]{1,0:T(8,128)S(1)} %get-tuple-element.335, f32[768]{0:T(1024)S(1)} %copy-done.90, f32[768]{0:T(1024)S(1)} %reshape.480, f32[704]{0:T(1024)S(1)} %add_rsqrt_fusion, ...), kind=kOutput, calls=%fused_computation.8 | convolution fusion | flops 3337568256 | bytes 19881472 | tf_op jit(solution)/shard_map/dot_general | solution.py:697
  213.7 9.7 %convert_reduce_fusion = (f32[3072]{0:T(1024)S(1)}, bf16[704,3072]{1,0:T(8,128)(2,1)S(1)}) fusion(f32[704,3072]{1,0:T(8,128)} %get-tuple-element.341, f32[3072]{0:T(1024)S(1)} %reshape.482, bf16[704,768]{1,0:T(8,128)(2,1)S(1)} %take.6, bf16[3072,768]{1,0:T(8,128)(2,1)S(1)} %bitcast.152), kind=kOutput, calls=%fused_computation.7 | convolution fusion | flops 3350000640 | bytes 18800640 | tf_op jit(solution)/shard_map/dot_general | solution.py:32
  223.4 4.1 multiply_reduce_fusion
  227.5 6.3 %convolution_convert_fusion.1 = bf16[768,3072]{1,0:T(8,128)(2,1)} fusion(bf16[704,3072]{1,0:T(8,128)(2,1)S(1)} %get-tuple-element.339, f32[704,768]{1,0:T(8,128)S(1)} %copy-done.64, f32[768]{0:T(1024)S(1)} %copy-done.90, f32[768]{0:T(1024)S(1)} %reshape.480, f32[704]{0:T(1024)S(1)} %add_rsqrt_fusion, f32[704]{0:T(1024)S(1)} %broadcast_multiply_fusion.4), kind=kOutput, calls=%fused_computation.13 | convolution fusion | flops 3326951424 | bytes 11218432 | tf_op jit(solution)/shard_map/dot_general | solution.py:36
  236.3 30.0 %attend_back.1 = (bf16[3,704,768]{2,1,0:T(8,128)(2,1)S(1)}, f32[4,128,128]{2,1,0:T(8,128)S(1)}, f32[6,8,128]{2,1,0:T(8,128)S(1)}) custom-call(bf16[704,2304]{1,0:T(8,128)(2,1)} %copy-done, bf16[704,2304]{1,0:T(8,128)(2,1)} %copy-done, bf16[704,2304]{1,0:T(8,128)(2,1)} %copy-done, bf16[704,768]{1,0:T(8,128)(2,1)S(1)} %convolution_convert_fusion.5.refs_3_, ...), custom_call_target="tpu_custom_call" | custom-call | tf_op jit(solution)/shard_map/attend_back/pallas_call | solution.py:240
  266.5 4.1 fusion.19
  274.8 5.1 %convolution_convert_fusion.2 = bf16[768,2304]{1,0:T(8,128)(2,1)} fusion(bf16[704,768]{1,0:T(8,128)(2,1)S(1)} %get-tuple-element.260, bf16[704,768]{1,0:T(8,128)(2,1)S(1)} %get-tuple-element.261, bf16[704,768]{1,0:T(8,128)(2,1)S(1)} %get-tuple-element.259, bf16[704,768]{1,0:T(8,128)(2,1)S(1)} %take.4, f32[768]{0:T(1024)S(1)} %copy-done.89, ...), kind=kOutput, calls=%fused_computation.14 | convolution fusion | flops 2506702848 | bytes 7876800 | tf_op jit(solution)/shard_map/dot_general | solution.py:36
  286.6 7.0 %convolution_convert_fusion = bf16[3072,768]{1,0:T(8,128)(2,1)S(1)} fusion(bf16[704,3072]{1,0:T(8,128)(2,1)} %get-tuple-element.340, bf16[704,768]{1,0:T(8,128)(2,1)S(1)} %take.6), kind=kOutput, calls=%fused_computation.12 | convolution fusion | flops 3324248064 | bytes 10125312 | tf_op jit(solution)/shard_map/dot_general | solution.py:36
  293.8 7.5 %add_convert_fusion.1.refs_1_.local_ref = bf16[704,768]{1,0:T(8,128)(2,1)S(1)} fusion(f32[704,768]{1,0:T(8,128)S(1)} %copy-done.65, bf16[704,3072]{1,0:T(8,128)(2,1)} %get-tuple-element.340, bf16[3072,768]{1,0:T(8,128)(2,1)S(1)} %bitcast.155, f32[768]{0:T(1024)S(1)} %copy-done.87), kind=kOutput, calls=%fused_computation.46 | convolution fusion | flops 3323510784 | bytes 12291072 | tf_op jit(solution)/shard_map/dot_general | solution.py:702
  314.6 2.6 collective-permute-start.86
  326.2 3.5 collective-permute-start.69
  331.7 2.5 collective-permute-done.91
  341.1 10.3 %collective-permute-start.59 = (bf16[176,768]{1,0:T(8,128)(2,1)}, bf16[176,768]{1,0:T(8,128)(2,1)S(1)}, u32[]{:S(2)}, u32[]{:S(2)}) collective-permute-start(bf16[176,768]{1,0:T(8,128)(2,1)} %get-tuple-element.143), channel_id=1, source_target_pairs={{3,2},{12,8},{7,6},{13,9},{15,11},{11,15},{14,10},{2,1},{0,3},{8,4... | collective-permute-start | bytes 811016 | tf_op jit(solution)/shard_map/ppermute | solution.py:475
  351.5 2.5 collective-permute-start.90
  359.3 3.6 take.7
  363.4 2.7 take.5
  367.5 3.8 collective-permute-start.95
  373.6 2.6 collective-permute-done.94
  382.1 2.4 collective-permute-done.75
  385.4 2.3 collective-permute-start.97
  390.1 3.9 collective-permute-done.78
  397.3 3.7 collective-permute-start.81
  401.6 2.2 collective-permute-done.79
  410.4 5.1 %collective-permute-done.107 = bf16[384,384]{1,0:T(8,128)(2,1)S(1)} collective-permute-done((bf16[384,384]{1,0:T(8,128)(2,1)S(1)}, bf16[384,384]{1,0:T(8,128)(2,1)S(1)}, u32[]{:S(2)}, u32[]{:S(2)}) %collective-permute-start.107) | collective-permute-done | bytes 294944 | tf_op jit(solution)/shard_map/ppermute | solution.py:486
  416.7 9.7 %collective-permute-done.100 = bf16[96,3072]{1,0:T(8,128)(2,1)S(1)} collective-permute-done((bf16[96,3072]{1,0:T(8,128)(2,1)S(1)}, bf16[96,3072]{1,0:T(8,128)(2,1)S(1)}, u32[]{:S(2)}, u32[]{:S(2)}) %collective-permute-start.100) | collective-permute-done | bytes 589856 | tf_op jit(solution)/shard_map/ppermute | solution.py:490
  428.7 3.8 collective-permute-start.103
  435.3 3.8 collective-permute-start.111
  439.1 7.5 %collective-permute-done.102 = bf16[24,3072]{1,0:T(8,128)(2,1)S(1)} collective-permute-done((bf16[24,3072]{1,0:T(8,128)(2,1)S(1)}, bf16[24,3072]{1,0:T(8,128)(2,1)S(1)}, u32[]{:S(2)}, u32[]{:S(2)}) %collective-permute-start.102) | collective-permute-done | bytes 147488 | tf_op jit(solution)/shard_map/ppermute | solution.py:498
  447.4 3.9 collective-permute-done.110
  (569 shorter events, 184.7 us)
Async XLA Ops:
  6.4 20.6 %collective-permute-start.6 = (bf16[32,288]{1,0:T(8,128)(2,1)S(1)}, bf16[32,288]{1,0:T(8,128)(2,1)S(1)}, u32[]{:S(2)}, u32[]{:S(2)}) collective-permute-start(bf16[32,288]{1,0:T(8,128)(2,1)S(1)} %broadcast_select_fusion.2), channel_id=1, source_target_pairs={{0,2},{1,3},{2,0},{3,1},{4,6},{5,7},{6,4},{7,5},{8,10},{9,11},{10,... | collective-permute-start | bytes 55304 | tf_op jit(solution)/shard_map/ppermute | solution.py:498
  10.4 16.6 %collective-permute-start.7 = (bf16[32,288]{1,0:T(8,128)(2,1)S(1)}, bf16[32,288]{1,0:T(8,128)(2,1)S(1)}, u32[]{:S(2)}, u32[]{:S(2)}) collective-permute-start(bf16[32,288]{1,0:T(8,128)(2,1)S(1)} %broadcast_select_fusion.2), channel_id=1, source_target_pairs={{0,3},{1,0},{2,1},{3,2},{4,7},{5,4},{6,5},{7,6},{8,11},{9,8},{10,9... | collective-permute-start | bytes 55304 | tf_op jit(solution)/shard_map/ppermute | solution.py:498
  11.8 16.6 %collective-permute-start.5 = (bf16[32,288]{1,0:T(8,128)(2,1)S(1)}, bf16[32,288]{1,0:T(8,128)(2,1)S(1)}, u32[]{:S(2)}, u32[]{:S(2)}) collective-permute-start(bf16[32,288]{1,0:T(8,128)(2,1)S(1)} %broadcast_select_fusion.2), channel_id=1, source_target_pairs={{0,1},{1,2},{2,3},{3,0},{4,5},{5,6},{6,7},{7,4},{8,9},{9,10},{10,1... | collective-permute-start | bytes 55304 | tf_op jit(solution)/shard_map/ppermute | solution.py:498
  12.4 24.9 %collective-permute-start.24 = (bf16[24,768]{1,0:T(8,128)(2,1)}, bf16[24,768]{1,0:T(8,128)(2,1)S(1)}, u32[]{:S(2)}, u32[]{:S(2)}) collective-permute-start(bf16[24,768]{1,0:T(8,128)(2,1)} %param.43), channel_id=1, source_target_pairs={{0,2},{1,3},{2,0},{3,1},{4,6},{5,7},{6,4},{7,5},{8,10},{9,11},{10,... | collective-permute-start | bytes 110600 | tf_op jit(solution)/shard_map/ppermute | solution.py:498
  13.5 24.2 %collective-permute-start.23 = (bf16[24,768]{1,0:T(8,128)(2,1)}, bf16[24,768]{1,0:T(8,128)(2,1)S(1)}, u32[]{:S(2)}, u32[]{:S(2)}) collective-permute-start(bf16[24,768]{1,0:T(8,128)(2,1)} %param.43), channel_id=1, source_target_pairs={{0,3},{1,0},{2,1},{3,2},{4,7},{5,4},{6,5},{7,6},{8,11},{9,8},{10,9... | collective-permute-start | bytes 110600 | tf_op jit(solution)/shard_map/ppermute | solution.py:498
  27.1 20.1 %collective-permute-start.12 = (bf16[24,2304]{1,0:T(8,128)(2,1)}, bf16[24,2304]{1,0:T(8,128)(2,1)S(1)}, u32[]{:S(2)}, u32[]{:S(2)}) collective-permute-start(bf16[24,2304]{1,0:T(8,128)(2,1)} %param.41), channel_id=1, source_target_pairs={{0,2},{1,3},{2,0},{3,1},{4,6},{5,7},{6,4},{7,5},{8,10},{9,11},{10,... | collective-permute-start | bytes 331784 | tf_op jit(solution)/shard_map/ppermute | solution.py:498
  34.5 18.2 %collective-permute-start.11 = (bf16[24,2304]{1,0:T(8,128)(2,1)S(1)}, bf16[24,2304]{1,0:T(8,128)(2,1)S(1)}, u32[]{:S(2)}, u32[]{:S(2)}) collective-permute-start(bf16[24,2304]{1,0:T(8,128)(2,1)S(1)} %copy-done.78), channel_id=1, source_target_pairs={{0,3},{1,0},{2,1},{3,2},{4,7},{5,4},{6,5},{7,6},{8,11},{9,8},{10,9... | collective-permute-start | bytes 331784 | tf_op jit(solution)/shard_map/ppermute | solution.py:498
  37.4 16.0 %collective-permute-start.13 = (bf16[24,2304]{1,0:T(8,128)(2,1)S(1)}, bf16[24,2304]{1,0:T(8,128)(2,1)S(1)}, u32[]{:S(2)}, u32[]{:S(2)}) collective-permute-start(bf16[24,2304]{1,0:T(8,128)(2,1)S(1)} %copy-done.78), channel_id=1, source_target_pairs={{0,1},{1,2},{2,3},{3,0},{4,5},{5,6},{6,7},{7,4},{8,9},{9,10},{10,1... | collective-permute-start | bytes 331784 | tf_op jit(solution)/shard_map/ppermute | solution.py:498
  45.1 16.2 %collective-permute-start.67 = (bf16[48,768]{1,0:T(8,128)(2,1)S(1)}, bf16[48,768]{1,0:T(8,128)(2,1)S(1)}, u32[]{:S(2)}, u32[]{:S(2)}) collective-permute-start(bf16[48,768]{1,0:T(8,128)(2,1)S(1)} %get-tuple-element.151), channel_id=1, source_target_pairs={{6,11},{9,14},{14,6},{5,10},{7,2},{13,12},{3,5},{4,9},{22,27},{25,... | collective-permute-start | bytes 221192 | tf_op jit(solution)/shard_map/ppermute | solution.py:469
  46.5 18.1 %collective-permute-start.66 = (bf16[80,768]{1,0:T(8,128)(2,1)S(1)}, bf16[80,768]{1,0:T(8,128)(2,1)S(1)}, u32[]{:S(2)}, u32[]{:S(2)}) collective-permute-start(bf16[80,768]{1,0:T(8,128)(2,1)S(1)} %get-tuple-element.150), channel_id=1, source_target_pairs={{9,10},{11,3},{14,12},{10,15},{7,11},{15,14},{3,7},{4,5},{12,13},{... | collective-permute-start | bytes 368648 | tf_op jit(solution)/shard_map/ppermute | solution.py:469
  65.3 16.4 %collective-permute-start.27 = (bf16[96,768]{1,0:T(8,128)(2,1)S(1)}, bf16[96,768]{1,0:T(8,128)(2,1)S(1)}, u32[]{:S(2)}, u32[]{:S(2)}) collective-permute-start(bf16[96,768]{1,0:T(8,128)(2,1)S(1)} %pad_maximum_fusion.14.refs_0_), channel_id=1, source_target_pairs={{0,8},{4,12},{8,0},{12,4},{1,9},{5,13},{9,1},{13,5},{2,10},{6,14},... | collective-permute-start | bytes 442376 | tf_op jit(solution)/shard_map/ppermute | solution.py:490
  65.9 17.0 %collective-permute-start.26 = (bf16[96,768]{1,0:T(8,128)(2,1)S(1)}, bf16[96,768]{1,0:T(8,128)(2,1)S(1)}, u32[]{:S(2)}, u32[]{:S(2)}) collective-permute-start(bf16[96,768]{1,0:T(8,128)(2,1)S(1)} %pad_maximum_fusion.14.refs_0_), channel_id=1, source_target_pairs={{0,16},{16,0},{1,17},{17,1},{2,18},{18,2},{3,19},{19,3},{4,20},{20... | collective-permute-start | bytes 442376 | tf_op jit(solution)/shard_map/ppermute | solution.py:486
  73.2 15.1 %collective-permute-start.47 = (bf16[96,768]{1,0:T(8,128)(2,1)}, bf16[96,768]{1,0:T(8,128)(2,1)S(1)}, u32[]{:S(2)}, u32[]{:S(2)}) collective-permute-start(bf16[96,768]{1,0:T(8,128)(2,1)} %param.51), channel_id=1, source_target_pairs={{0,3},{1,0},{2,1},{3,2},{4,7},{5,4},{6,5},{7,6},{8,11},{9,8},{10,9... | collective-permute-start | bytes 442376 | tf_op jit(solution)/shard_map/ppermute | solution.py:498
  84.1 20.6 %collective-permute-start.64 = (bf16[176,768]{1,0:T(8,128)(2,1)}, bf16[176,768]{1,0:T(8,128)(2,1)S(1)}, u32[]{:S(2)}, u32[]{:S(2)}) collective-permute-start(bf16[176,768]{1,0:T(8,128)(2,1)} %get-tuple-element.148), channel_id=1, source_target_pairs={{2,3},{8,12},{6,7},{9,13},{11,15},{15,11},{10,14},{1,2},{3,0},{4,8... | collective-permute-start | bytes 811016 | tf_op jit(solution)/shard_map/ppermute | solution.py:469
  89.6 24.4 %collective-permute-start.15 = (bf16[96,2304]{1,0:T(8,128)(2,1)}, bf16[96,2304]{1,0:T(8,128)(2,1)}, u32[]{:S(2)}, u32[]{:S(2)}) collective-permute-start(bf16[96,2304]{1,0:T(8,128)(2,1)} %pad_maximum_fusion.11.refs_0_), channel_id=1, source_target_pairs={{0,8},{4,12},{8,0},{12,4},{1,9},{5,13},{9,1},{13,5},{2,10},{6,14},... | collective-permute-start | bytes 1327112 | tf_op jit(solution)/shard_map/ppermute | solution.py:490
  108.0 17.3 %collective-permute-start.14 = (bf16[96,2304]{1,0:T(8,128)(2,1)}, bf16[96,2304]{1,0:T(8,128)(2,1)}, u32[]{:S(2)}, u32[]{:S(2)}) collective-permute-start(bf16[96,2304]{1,0:T(8,128)(2,1)} %pad_maximum_fusion.11.refs_0_), channel_id=1, source_target_pairs={{0,16},{16,0},{1,17},{17,1},{2,18},{18,2},{3,19},{19,3},{4,20},{20... | collective-permute-start | bytes 1327112 | tf_op jit(solution)/shard_map/ppermute | solution.py:486
  109.2 19.1 %collective-permute-start.51 = (bf16[384,768]{1,0:T(8,128)(2,1)S(1)}, bf16[384,768]{1,0:T(8,128)(2,1)}, u32[]{:S(2)}, u32[]{:S(2)}) collective-permute-start(bf16[384,768]{1,0:T(8,128)(2,1)S(1)} %pad_maximum_fusion.5.refs_0_), channel_id=1, source_target_pairs={{0,8},{4,12},{8,0},{12,4},{1,9},{5,13},{9,1},{13,5},{2,10},{6,14},... | collective-permute-start | bytes 1769480 | tf_op jit(solution)/shard_map/ppermute | solution.py:490
  111.6 22.3 %collective-permute-start.50 = (bf16[384,768]{1,0:T(8,128)(2,1)S(1)}, bf16[384,768]{1,0:T(8,128)(2,1)}, u32[]{:S(2)}, u32[]{:S(2)}) collective-permute-start(bf16[384,768]{1,0:T(8,128)(2,1)S(1)} %pad_maximum_fusion.5.refs_0_), channel_id=1, source_target_pairs={{0,16},{16,0},{1,17},{17,1},{2,18},{18,2},{3,19},{19,3},{4,20},{20... | collective-permute-start | bytes 1769480 | tf_op jit(solution)/shard_map/ppermute | solution.py:486
  113.7 24.4 %collective-permute-start.39 = (bf16[96,3072]{1,0:T(8,128)(2,1)S(1)}, bf16[96,3072]{1,0:T(8,128)(2,1)}, u32[]{:S(2)}, u32[]{:S(2)}) collective-permute-start(bf16[96,3072]{1,0:T(8,128)(2,1)S(1)} %pad_maximum_fusion.4.refs_0_), channel_id=1, source_target_pairs={{0,8},{4,12},{8,0},{12,4},{1,9},{5,13},{9,1},{13,5},{2,10},{6,14},... | collective-permute-start | bytes 1769480 | tf_op jit(solution)/shard_map/ppermute | solution.py:490
  114.0 32.6 %collective-permute-start.38 = (bf16[96,3072]{1,0:T(8,128)(2,1)S(1)}, bf16[96,3072]{1,0:T(8,128)(2,1)}, u32[]{:S(2)}, u32[]{:S(2)}) collective-permute-start(bf16[96,3072]{1,0:T(8,128)(2,1)S(1)} %pad_maximum_fusion.4.refs_0_), channel_id=1, source_target_pairs={{0,16},{16,0},{1,17},{17,1},{2,18},{18,2},{3,19},{19,3},{4,20},{20... | collective-permute-start | bytes 1769480 | tf_op jit(solution)/shard_map/ppermute | solution.py:486
  127.7 29.0 %collective-permute-start.18 = (bf16[96,2304]{1,0:T(8,128)(2,1)}, bf16[96,2304]{1,0:T(8,128)(2,1)S(1)}, u32[]{:S(2)}, u32[]{:S(2)}) collective-permute-start(bf16[96,2304]{1,0:T(8,128)(2,1)} %pad_maximum_fusion.11.refs_0_), channel_id=1, source_target_pairs={{0,4},{4,0},{8,12},{12,8},{1,5},{5,1},{9,13},{13,9},{2,6},{6,2},{1... | collective-permute-start | bytes 1327112 | tf_op jit(solution)/shard_map/ppermute | solution.py:494
  128.3 22.1 %collective-permute-start.16 = (bf16[96,1152]{1,0:T(8,128)(2,1)S(1)}, bf16[96,1152]{1,0:T(8,128)(2,1)S(1)}, u32[]{:S(2)}, u32[]{:S(2)}) collective-permute-start(bf16[96,1152]{1,0:T(8,128)(2,1)S(1)} %slice.453), channel_id=1, source_target_pairs={{0,16},{16,0},{1,17},{17,1},{2,18},{18,2},{3,19},{19,3},{4,20},{20... | collective-permute-start | bytes 663560 | tf_op jit(solution)/shard_map/ppermute | solution.py:486
  133.9 16.5 %collective-permute-start.17 = (bf16[96,1152]{1,0:T(8,128)(2,1)S(1)}, bf16[96,1152]{1,0:T(8,128)(2,1)S(1)}, u32[]{:S(2)}, u32[]{:S(2)}) collective-permute-start(bf16[96,1152]{1,0:T(8,128)(2,1)S(1)} %slice.454), channel_id=1, source_target_pairs={{0,8},{4,12},{8,0},{12,4},{1,9},{5,13},{9,1},{13,5},{2,10},{6,14},... | collective-permute-start | bytes 663560 | tf_op jit(solution)/shard_map/ppermute | solution.py:490
  138.1 19.3 %collective-permute-start.20 = (bf16[96,2304]{1,0:T(8,128)(2,1)}, bf16[96,2304]{1,0:T(8,128)(2,1)S(1)}, u32[]{:S(2)}, u32[]{:S(2)}) collective-permute-start(bf16[96,2304]{1,0:T(8,128)(2,1)} %collective-permute-done.15.refs_2_), channel_id=1, source_target_pairs={{0,4},{4,0},{8,12},{12,8},{1,5},{5,1},{9,13},{13,9},{2,6},{6,2},{1... | collective-permute-start | bytes 1327112 | tf_op jit(solution)/shard_map/ppermute | solution.py:494
  156.7 29.5 %collective-permute-start.42 = (bf16[96,3072]{1,0:T(8,128)(2,1)S(1)}, bf16[96,3072]{1,0:T(8,128)(2,1)S(1)}, u32[]{:S(2)}, u32[]{:S(2)}) collective-permute-start(bf16[96,3072]{1,0:T(8,128)(2,1)S(1)} %copy-done.8), channel_id=1, source_target_pairs={{0,4},{4,0},{8,12},{12,8},{1,5},{5,1},{9,13},{13,9},{2,6},{6,2},{1... | collective-permute-start | bytes 1769480 | tf_op jit(solution)/shard_map/ppermute | solution.py:494
  156.8 30.0 %collective-permute-start.52 = (bf16[384,384]{1,0:T(8,128)(2,1)S(1)}, bf16[384,384]{1,0:T(8,128)(2,1)S(1)}, u32[]{:S(2)}, u32[]{:S(2)}) collective-permute-start(bf16[384,384]{1,0:T(8,128)(2,1)S(1)} %slice.466), channel_id=1, source_target_pairs={{0,16},{16,0},{1,17},{17,1},{2,18},{18,2},{3,19},{19,3},{4,20},{20... | collective-permute-start | bytes 884744 | tf_op jit(solution)/shard_map/ppermute | solution.py:486
  157.4 30.1 %collective-permute-start.40 = (bf16[96,1536]{1,0:T(8,128)(2,1)S(1)}, bf16[96,1536]{1,0:T(8,128)(2,1)S(1)}, u32[]{:S(2)}, u32[]{:S(2)}) collective-permute-start(bf16[96,1536]{1,0:T(8,128)(2,1)S(1)} %slice.463), channel_id=1, source_target_pairs={{0,16},{16,0},{1,17},{17,1},{2,18},{18,2},{3,19},{19,3},{4,20},{20... | collective-permute-start | bytes 884744 | tf_op jit(solution)/shard_map/ppermute | solution.py:486
  158.9 28.6 %collective-permute-start.41 = (bf16[96,1536]{1,0:T(8,128)(2,1)S(1)}, bf16[96,1536]{1,0:T(8,128)(2,1)S(1)}, u32[]{:S(2)}, u32[]{:S(2)}) collective-permute-start(bf16[96,1536]{1,0:T(8,128)(2,1)S(1)} %slice.464), channel_id=1, source_target_pairs={{0,8},{4,12},{8,0},{12,4},{1,9},{5,13},{9,1},{13,5},{2,10},{6,14},... | collective-permute-start | bytes 884744 | tf_op jit(solution)/shard_map/ppermute | solution.py:490
  160.2 35.6 %collective-permute-start.44 = (bf16[96,3072]{1,0:T(8,128)(2,1)}, bf16[96,3072]{1,0:T(8,128)(2,1)S(1)}, u32[]{:S(2)}, u32[]{:S(2)}) collective-permute-start(bf16[96,3072]{1,0:T(8,128)(2,1)} %collective-permute-done.39.refs_2_), channel_id=1, source_target_pairs={{0,4},{4,0},{8,12},{12,8},{1,5},{5,1},{9,13},{13,9},{2,6},{6,2},{1... | collective-permute-start | bytes 1769480 | tf_op jit(solution)/shard_map/ppermute | solution.py:494
  195.8 15.6 %collective-permute-start.54 = (bf16[384,768]{1,0:T(8,128)(2,1)S(1)}, bf16[384,768]{1,0:T(8,128)(2,1)S(1)}, u32[]{:S(2)}, u32[]{:S(2)}) collective-permute-start(bf16[384,768]{1,0:T(8,128)(2,1)S(1)} %copy-done.10), channel_id=1, source_target_pairs={{0,4},{4,0},{8,12},{12,8},{1,5},{5,1},{9,13},{13,9},{2,6},{6,2},{1... | collective-permute-start | bytes 1769480 | tf_op jit(solution)/shard_map/ppermute | solution.py:494
  281.2 27.5 %collective-permute-start.84 = (f32[12672]{0:T(1024)}, f32[12672]{0:T(1024)}, u32[]{:S(2)}, u32[]{:S(2)}) collective-permute-start(f32[12672]{0:T(1024)} %concatenate.129), channel_id=1, source_target_pairs={{0,3},{1,0},{2,1},{3,2},{4,7},{5,4},{6,5},{7,6},{8,11},{9,8},{10,9... | collective-permute-start | bytes 152072 | tf_op jit(solution)/shard_map/ppermute | solution.py:498
  282.7 26.6 %collective-permute-start.83 = (f32[12672]{0:T(1024)}, f32[12672]{0:T(1024)}, u32[]{:S(2)}, u32[]{:S(2)}) collective-permute-start(f32[12672]{0:T(1024)} %concatenate.129), channel_id=1, source_target_pairs={{0,2},{1,3},{2,0},{3,1},{4,6},{5,7},{6,4},{7,5},{8,10},{9,11},{10,... | collective-permute-start | bytes 152072 | tf_op jit(solution)/shard_map/ppermute | solution.py:498
  284.6 24.8 %collective-permute-start.82 = (f32[12672]{0:T(1024)}, f32[12672]{0:T(1024)}, u32[]{:S(2)}, u32[]{:S(2)}) collective-permute-start(f32[12672]{0:T(1024)} %concatenate.129), channel_id=1, source_target_pairs={{0,1},{1,2},{2,3},{3,0},{4,5},{5,6},{6,7},{7,4},{8,9},{9,10},{10,1... | collective-permute-start | bytes 152072 | tf_op jit(solution)/shard_map/ppermute | solution.py:498
  301.4 17.9 %collective-permute-start.88 = (bf16[4,96,768]{2,1,0:T(8,128)(2,1)S(1)}, bf16[4,96,768]{2,1,0:T(8,128)(2,1)S(1)}, u32[]{:S(2)}, u32[]{:S(2)}) collective-permute-start(bf16[4,96,768]{2,1,0:T(8,128)(2,1)S(1)} %pad_maximum_fusion.6), channel_id=1, source_target_pairs={{0,4},{4,0},{8,12},{12,8},{1,5},{5,1},{9,13},{13,9},{2,6},{6,2},{1... | collective-permute-start | bytes 1769480 | tf_op jit(solution)/shard_map/ppermute | solution.py:494
  305.5 24.9 %collective-permute-start.73 = (bf16[32,768]{1,0:T(8,128)(2,1)S(1)}, bf16[32,768]{1,0:T(8,128)(2,1)S(1)}, u32[]{:S(2)}, u32[]{:S(2)}) collective-permute-start(bf16[32,768]{1,0:T(8,128)(2,1)S(1)} %get-tuple-element.159), channel_id=1, source_target_pairs={{10,13},{6,1},{9,12},{5,0},{26,29},{22,17},{25,28},{21,16}} | collective-permute-start | bytes 147464 | tf_op jit(solution)/shard_map/ppermute | solution.py:475
  308.6 27.9 %collective-permute-start.72 = (bf16[48,768]{1,0:T(8,128)(2,1)S(1)}, bf16[48,768]{1,0:T(8,128)(2,1)S(1)}, u32[]{:S(2)}, u32[]{:S(2)}) collective-permute-start(bf16[48,768]{1,0:T(8,128)(2,1)S(1)} %get-tuple-element.158), channel_id=1, source_target_pairs={{11,6},{14,9},{6,14},{10,5},{2,7},{12,13},{5,3},{9,4},{27,22},{30,... | collective-permute-start | bytes 221192 | tf_op jit(solution)/shard_map/ppermute | solution.py:475
  309.3 62.0 %collective-permute-start.74 = (bf16[4,96,2304]{2,1,0:T(8,128)(2,1)}, bf16[4,96,2304]{2,1,0:T(8,128)(2,1)}, u32[]{:S(2)}, u32[]{:S(2)}) collective-permute-start(bf16[4,96,2304]{2,1,0:T(8,128)(2,1)} %pad_maximum_fusion.3), channel_id=1, source_target_pairs={{0,4},{4,0},{8,12},{12,8},{1,5},{5,1},{9,13},{13,9},{2,6},{6,2},{1... | collective-permute-start | bytes 5308424 | tf_op jit(solution)/shard_map/ppermute | solution.py:494
  326.2 25.3 %collective-permute-start.69 = (bf16[176,768]{1,0:T(8,128)(2,1)S(1)}, bf16[176,768]{1,0:T(8,128)(2,1)S(1)}, u32[]{:S(2)}, u32[]{:S(2)}) collective-permute-start(bf16[176,768]{1,0:T(8,128)(2,1)S(1)} %get-tuple-element.155), channel_id=1, source_target_pairs={{3,2},{12,8},{7,6},{13,9},{15,11},{11,15},{14,10},{2,1},{0,3},{8,4... | collective-permute-start | bytes 811016 | tf_op jit(solution)/shard_map/ppermute | solution.py:475
  339.8 23.1 %collective-permute-start.60 = (bf16[128,768]{1,0:T(8,128)(2,1)}, bf16[128,768]{1,0:T(8,128)(2,1)S(1)}, u32[]{:S(2)}, u32[]{:S(2)}) collective-permute-start(bf16[128,768]{1,0:T(8,128)(2,1)} %get-tuple-element.144), channel_id=1, source_target_pairs={{11,10},{1,3},{8,12},{9,5},{15,14},{10,6},{2,11},{14,13},{6,15},{4... | collective-permute-start | bytes 589832 | tf_op jit(solution)/shard_map/ppermute | solution.py:475
  341.1 21.8 %collective-permute-start.59 = (bf16[176,768]{1,0:T(8,128)(2,1)}, bf16[176,768]{1,0:T(8,128)(2,1)S(1)}, u32[]{:S(2)}, u32[]{:S(2)}) collective-permute-start(bf16[176,768]{1,0:T(8,128)(2,1)} %get-tuple-element.143), channel_id=1, source_target_pairs={{3,2},{12,8},{7,6},{13,9},{15,11},{11,15},{14,10},{2,1},{0,3},{8,4... | collective-permute-start | bytes 811016 | tf_op jit(solution)/shard_map/ppermute | solution.py:475
  362.9 26.7 %collective-permute-start.104 = (bf16[4,384,768]{2,1,0:T(8,128)(2,1)}, bf16[4,384,768]{2,1,0:T(8,128)(2,1)S(1)}, u32[]{:S(2)}, u32[]{:S(2)}) collective-permute-start(bf16[4,384,768]{2,1,0:T(8,128)(2,1)} %pad_maximum_fusion.2), channel_id=1, source_target_pairs={{0,4},{4,0},{8,12},{12,8},{1,5},{5,1},{9,13},{13,9},{2,6},{6,2},{1... | collective-permute-start | bytes 7077896 | tf_op jit(solution)/shard_map/ppermute | solution.py:494
  362.9 21.8 %collective-permute-start.96 = (bf16[4,96,3072]{2,1,0:T(8,128)(2,1)S(1)}, bf16[4,96,3072]{2,1,0:T(8,128)(2,1)S(1)}, u32[]{:S(2)}, u32[]{:S(2)}) collective-permute-start(bf16[4,96,3072]{2,1,0:T(8,128)(2,1)S(1)} %copy-done.72), channel_id=1, source_target_pairs={{0,4},{4,0},{8,12},{12,8},{1,5},{5,1},{9,13},{13,9},{2,6},{6,2},{1... | collective-permute-start | bytes 7077896 | tf_op jit(solution)/shard_map/ppermute | solution.py:494
  385.4 24.6 %collective-permute-start.97 = (bf16[96,1536]{1,0:T(8,128)(2,1)S(1)}, bf16[96,1536]{1,0:T(8,128)(2,1)S(1)}, u32[]{:S(2)}, u32[]{:S(2)}) collective-permute-start(bf16[96,1536]{1,0:T(8,128)(2,1)S(1)} %get-tuple-element.278), channel_id=1, source_target_pairs={{0,8},{4,12},{8,0},{12,4},{1,9},{5,13},{9,1},{13,5},{2,10},{6,14},... | collective-permute-start | bytes 884744 | tf_op jit(solution)/shard_map/ppermute | solution.py:490
  387.7 20.3 %collective-permute-start.99 = (bf16[96,1536]{1,0:T(8,128)(2,1)S(1)}, bf16[96,1536]{1,0:T(8,128)(2,1)S(1)}, u32[]{:S(2)}, u32[]{:S(2)}) collective-permute-start(bf16[96,1536]{1,0:T(8,128)(2,1)S(1)} %get-tuple-element.279), channel_id=1, source_target_pairs={{0,16},{16,0},{1,17},{17,1},{2,18},{18,2},{3,19},{19,3},{4,20},{20... | collective-permute-start | bytes 884744 | tf_op jit(solution)/shard_map/ppermute | solution.py:486
  408.1 18.3 %collective-permute-start.100 = (bf16[96,3072]{1,0:T(8,128)(2,1)S(1)}, bf16[96,3072]{1,0:T(8,128)(2,1)S(1)}, u32[]{:S(2)}, u32[]{:S(2)}) collective-permute-start(bf16[96,3072]{1,0:T(8,128)(2,1)S(1)} %pad_maximum_fusion.8), channel_id=1, source_target_pairs={{0,8},{4,12},{8,0},{12,4},{1,9},{5,13},{9,1},{13,5},{2,10},{6,14},... | collective-permute-start | bytes 1769480 | tf_op jit(solution)/shard_map/ppermute | solution.py:490
  410.1 18.1 %collective-permute-start.98 = (bf16[96,3072]{1,0:T(8,128)(2,1)S(1)}, bf16[96,3072]{1,0:T(8,128)(2,1)S(1)}, u32[]{:S(2)}, u32[]{:S(2)}) collective-permute-start(bf16[96,3072]{1,0:T(8,128)(2,1)S(1)} %pad_maximum_fusion.7), channel_id=1, source_target_pairs={{0,16},{16,0},{1,17},{17,1},{2,18},{18,2},{3,19},{19,3},{4,20},{20... | collective-permute-start | bytes 1769480 | tf_op jit(solution)/shard_map/ppermute | solution.py:486
  415.7 17.5 %collective-permute-start.108 = (bf16[384,768]{1,0:T(8,128)(2,1)S(1)}, bf16[384,768]{1,0:T(8,128)(2,1)S(1)}, u32[]{:S(2)}, u32[]{:S(2)}) collective-permute-start(bf16[384,768]{1,0:T(8,128)(2,1)S(1)} %pad_maximum_fusion.10), channel_id=1, source_target_pairs={{0,8},{4,12},{8,0},{12,4},{1,9},{5,13},{9,1},{13,5},{2,10},{6,14},... | collective-permute-start | bytes 1769480 | tf_op jit(solution)/shard_map/ppermute | solution.py:490
  416.1 18.7 %collective-permute-start.106 = (bf16[384,768]{1,0:T(8,128)(2,1)S(1)}, bf16[384,768]{1,0:T(8,128)(2,1)S(1)}, u32[]{:S(2)}, u32[]{:S(2)}) collective-permute-start(bf16[384,768]{1,0:T(8,128)(2,1)S(1)} %pad_maximum_fusion.9), channel_id=1, source_target_pairs={{0,16},{16,0},{1,17},{17,1},{2,18},{18,2},{3,19},{19,3},{4,20},{20... | collective-permute-start | bytes 1769480 | tf_op jit(solution)/shard_map/ppermute | solution.py:486
  (166 other events, 1824.2 us)
